TPU v7x, 32 devices: a whole 2x2x4 slice. The times are simulated.
32 devices in a mesh: mem: 8 (over z, x), fsdp: 4 (over y, core).
Axes of the slice: x: 2, y: 2, z: 4, core: 2. Of those that a mesh axis runs over, the one named last changes fastest.
Arguments:
- layer_input: bfloat16 [4096, 4096], P(('mem', 'fsdp')), may hold values from -6 to 6
- w_query: bfloat16 [4096, 2048], P('mem', 'fsdp'), may hold values from -0.09375 to 0.09375
- local_kv: bfloat16 [2, 4096, 2048], P(None, 'mem', 'fsdp'), may hold values from -200 to 200, as said below
- memory_kv: bfloat16 [128, 2, 128, 2048], P('mem', None, None, 'fsdp'), may hold values from -200 to 200
- memory_ids: int32 [32, 4], P('mem'), may hold values from 0 to 127, as said below
- grad_out: bfloat16 [4096, 2048], P('mem', 'fsdp'), may hold values from -6 to 6
Outputs:
- attended: bfloat16 [4096, 2048], P('mem', 'fsdp')
- grad_input: bfloat16 [4096, 4096], P(('mem', 'fsdp'))
Inputs may be any that keep to these rules, and one draw needn't show every extreme that they name: `memory_ids`: within the tiles of one local context (4 tiles), all named blocks of one owner (same id // 16) are one and the same block, and every owner is named by some tile of every local context; each tile names 4 blocks of different owners. `local_kv`: keys and values of the document's tokens.
All inputs are finite; a program needn't handle non-finite values.
Results may differ from a plain program's by a relative error of at most 0.025.
The roundings to bfloat16 on the way count: a program that leaves them out, or rounds other values in their place, can miss the bound.
Values may be sent and summed in bfloat16 or wider, within the bound.
A program may use at most 128 MiB of HBM per device.

v0:
```python
import functools
import math

import jax
import jax.numpy as jnp
from jax import lax
from jax.experimental import pallas as pl
from jax.experimental.pallas import tpu as pltpu
from jax.sharding import PartitionSpec as P

HD = 128
BLK = 128
NEG_FILL = -1e30
MESH = pl.DeviceIdType.MESH
NT = (((1,), (1,)), ((), ()))


def dot_nn(a, b):
    return jnp.dot(a, b, preferred_element_type=jnp.float32)


def dot_nt(a, b):
    return lax.dot_general(a, b, NT, preferred_element_type=jnp.float32)


def kernel(
    n, nx, nf, topk, mb_dev, pre, parts,
    ids_s, ids_v, x_hbm, w_hbm, lkv_hbm, mkv_hbm, go_hbm,
    att_ref, gin_ref,
    wf, xf, kv, lkv, go, outbox, inbox, ids_in, ids_sm, q32, qb, gq,
    p_send, p_own, s_recv, y_send, y_recv, s_loc, d_loc,
    l_sem, i_send, i_recv, i_loc, w_up, w_down, w_x, w_recv, wx_recv,
    x_ysend, x_ssend, x_recv, m_send, m_recv, r_ssend, r_srecv, r_ysend, r_yrecv,
):
    me = lax.axis_index("mem")
    mf = lax.axis_index("fsdp")
    nz = n // nx
    z, xx = me // nx, lax.rem(me, nx)
    ny = nf // 2
    yy, cc = mf // 2, lax.rem(mf, 2)
    sib = mf + 1 - 2 * cc
    dk = wf.shape[1]
    width = wf.shape[2]
    heads = width // HD
    tiles = ids_s.shape[0]
    rows_dev = xf.shape[0] // nf
    ctx = xf.shape[0]

    def local_copy(src, dst, k):
        return pltpu.make_async_copy(src, dst, l_sem.at[k])

    own_x = pl.ds(pl.multiple_of(mf * rows_dev, rows_dev), rows_dev)
    c_w = local_copy(w_hbm, wf.at[me], 0)
    c_x = local_copy(x_hbm, xf.at[own_x, :], 1)
    c_kv = local_copy(mkv_hbm, kv, 2)
    c_lkv = local_copy(lkv_hbm, lkv, 3)
    c_go = local_copy(go_hbm, go, 4)
    c_w.start()
    c_x.start()
    c_kv.start()
    c_lkv.start()
    c_go.start()

    barrier = pltpu.get_barrier_semaphore()

    @pl.loop(1, n)
    def _(d):
        pl.semaphore_signal(
            barrier, inc=1, device_id=(lax.rem(me + d, n), mf), device_id_type=MESH
        )

    pl.semaphore_signal(barrier, inc=1, device_id=(me, sib), device_id_type=MESH)
    for d in range(1, ny):
        pl.semaphore_signal(
            barrier, inc=1, device_id=(me, lax.rem(mf + 2 * d, nf)), device_id_type=MESH
        )
    pl.semaphore_wait(barrier, n - 1 + 1 + ny - 1)

    def remote(src, dst, s, r, dm, df):
        return pltpu.make_async_remote_copy(
            src_ref=src, dst_ref=dst, send_sem=s, recv_sem=r,
            device_id=(dm, df), device_id_type=MESH,
        )

    def id_copy(peer, slot):
        return remote(ids_v, inbox.at[slot], i_send.at[peer], i_recv.at[slot], peer, mf)

    @pl.loop(1, n)
    def _(d):
        id_copy(lax.rem(me + d, n), me).start()

    def w_copy(slot, sem, dst_m, rsem):
        return remote(wf.at[slot], wf.at[slot], sem, rsem, dst_m, mf)

    def w_up_copy(zz):
        return w_copy(zz * nx + xx, w_up.at[zz], me + nx, w_recv.at[zz])

    def w_down_copy(zz):
        return w_copy(zz * nx + xx, w_down.at[zz], me - nx, w_recv.at[zz])

    x_next = z * nx + lax.rem(xx + 1, nx)

    def w_x_copy(r, zz):
        slot = zz * nx + lax.rem(xx - r + nx, nx)
        return w_copy(slot, w_x.at[r, zz], x_next, wx_recv.at[r, zz])

    def w_x_arrival(r, zz):
        slot = zz * nx + lax.rem(xx - 1 - r + 2 * nx, nx)
        return w_copy(slot, w_x.at[r, zz], x_next, wx_recv.at[r, zz])

    c_w.wait()

    @pl.when(z + 1 < nz)
    def _():
        w_up_copy(z).start()

    @pl.when(z > 0)
    def _():
        w_down_copy(z).start()

    w_x_copy(0, z).start()
    c_x.wait()

    def x_rows(f):
        return xf.at[pl.ds(pl.multiple_of(f * rows_dev, rows_dev), rows_dev), :]

    def x_ycopy(d):
        return remote(
            x_rows(mf), x_rows(mf), x_ysend.at[d], x_recv.at[mf], me, lax.rem(mf + 2 * d, nf)
        )

    def x_scopy(f):
        return remote(x_rows(f), x_rows(f), x_ssend.at[f], x_recv.at[f], me, sib)

    for d in range(1, ny):
        x_ycopy(d).start()
    x_scopy(mf).start()

    @pl.loop(1, n)
    def _(d):
        src = lax.rem(me + d, n)
        id_copy(src, src).wait_recv()

    c_ids = pltpu.make_async_copy(inbox, ids_sm, i_loc.at[0])
    c_ids.start()
    c_kv.wait()
    c_ids.wait()

    @pl.loop(1, n)
    def _(d):
        peer = lax.rem(me + d, n)
        want = jnp.int32(0)
        for j in range(tiles * topk):
            one = ids_sm[peer, 0, j]
            want = jnp.where(one // mb_dev == me, lax.rem(one, mb_dev), want)
        outbox[peer] = kv[want]

    mine = jnp.int32(0)
    for j in range(tiles * topk):
        one = ids_s[j // topk, j % topk]
        mine = jnp.where(one // mb_dev == me, lax.rem(one, mb_dev), mine)
    ids_in[me] = kv[mine]

    def block_copy(peer, slot):
        return remote(
            outbox.at[peer], ids_in.at[slot], m_send.at[peer], m_recv.at[slot], peer, mf
        )

    def send_blocks(k):
        @pl.loop(1, n)
        def _(d):
            peer = lax.rem(me + n - d, n)
            column = lax.rem(peer, nx) == xx

            @pl.when((column & (k == 3)) | (jnp.logical_not(column) & (k == 2)))
            def _():
                block_copy(peer, me).start()

    for k in range(1, nz):
        @pl.when(z - k >= 0)
        def _():
            w_up_copy(z - k).wait_recv()

            @pl.when(z + 1 < nz)
            def _():
                w_up_copy(z - k).start()

            w_x_copy(0, z - k).start()

        @pl.when(z + k < nz)
        def _():
            w_down_copy(z + k).wait_recv()

            @pl.when(z > 0)
            def _():
                w_down_copy(z + k).start()

            w_x_copy(0, z + k).start()

        send_blocks(k)

    for d in range(1, ny):
        f = lax.rem(mf + 2 * d, nf)
        x_scopy(f).wait_recv()
        x_scopy(f).start()
    for d in range(ny):
        x_scopy(lax.rem(sib + 2 * d, nf)).wait_recv()

    q32[...] = jnp.zeros_like(q32)

    def project(slot):
        q32[...] += dot_nn(xf[:, pl.ds(pl.multiple_of(slot * dk, dk), dk)], wf[slot])

    def by_distance(body):
        body(z)
        for k in range(1, nz):
            for zz in (z - k, z + k):
                @pl.when((zz >= 0) & (zz < nz))
                def _():
                    body(zz)

    @pl.loop(0, nz)
    def _(zz):
        project(zz * nx + xx)

    for r in range(nx - 1):
        def arrived(zz):
            w_x_arrival(r, zz).wait_recv()
            if r + 1 < nx - 1:
                w_x_copy(r + 1, zz).start()
            project(zz * nx + lax.rem(xx - 1 - r + 2 * nx, nx))

        by_distance(arrived)

    qb[...] = q32[...].astype(jnp.bfloat16)
    c_lkv.wait()
    c_go.wait()

    scale = 1.0 / math.sqrt(HD)

    def head_cols(h):
        return pl.ds(pl.multiple_of(h * HD, HD), HD)

    if pre:
        @pl.loop(0, heads)
        def _(h):
            cols = head_cols(h)
            causal = lax.broadcasted_iota(jnp.int32, (ctx, ctx), 0) >= (
                lax.broadcasted_iota(jnp.int32, (ctx, ctx), 1)
            )
            s_loc[h] = jnp.where(causal, dot_nt(qb[:, cols], lkv[0, :, cols]) * scale, NEG_FILL)
            d_loc[h] = dot_nt(go[:, cols], lkv[1, :, cols])

    @pl.loop(1, n)
    def _(d):
        src = lax.rem(me + d, n)
        block_copy(src, src).wait_recv()

    def attend(t):
        rows = pl.ds(pl.multiple_of(t * BLK, BLK), BLK)
        owners = [ids_s[t, j] // mb_dev for j in range(topk)]

        @pl.loop(0, heads)
        def _(h):
            cols = head_cols(h)
            mk = jnp.concatenate([ids_in[o, 0, :, cols] for o in owners], axis=0)
            mv = jnp.concatenate([ids_in[o, 1, :, cols] for o in owners], axis=0)
            lk = lkv[0, :, cols]
            lv = lkv[1, :, cols]
            if pre:
                s_m = dot_nt(qb[rows, cols], mk) * scale
                d_m = dot_nt(go[rows, cols], mv)
                s_l = s_loc[h, rows, :]
                d_l = d_loc[h, rows, :]
            else:
                q = qb[rows, cols]
                g = go[rows, cols]
                causal = lax.broadcasted_iota(jnp.int32, (BLK, ctx), 0) + t * BLK >= (
                    lax.broadcasted_iota(jnp.int32, (BLK, ctx), 1)
                )
                s_m = dot_nt(q, mk) * scale
                s_l = jnp.where(causal, dot_nt(q, lk) * scale, NEG_FILL)
                d_m = dot_nt(g, mv)
                d_l = dot_nt(g, lv)
            top = jnp.maximum(
                jnp.max(s_m, axis=1, keepdims=True), jnp.max(s_l, axis=1, keepdims=True)
            )
            e_m = jnp.exp(s_m - top)
            e_l = jnp.exp(s_l - top)
            inv = 1.0 / (
                jnp.sum(e_m, axis=1, keepdims=True) + jnp.sum(e_l, axis=1, keepdims=True)
            )
            p_m = e_m * inv
            p_l = e_l * inv
            att_ref[rows, cols] = (
                dot_nn(p_m.astype(jnp.bfloat16), mv) + dot_nn(p_l.astype(jnp.bfloat16), lv)
            ).astype(jnp.bfloat16)
            delta = jnp.sum(p_m * d_m, axis=1, keepdims=True) + jnp.sum(
                p_l * d_l, axis=1, keepdims=True
            )
            ds_m = (p_m * (d_m - delta)).astype(jnp.bfloat16)
            ds_l = (p_l * (d_l - delta)).astype(jnp.bfloat16)
            gq[rows, cols] = ((dot_nn(ds_m, mk) + dot_nn(ds_l, lk)) * scale).astype(jnp.bfloat16)

    per = n // parts

    def shards(p):
        return pl.ds(p * per, per)

    def rs_s(d, p):
        return remote(
            p_send.at[d, shards(p)], s_recv.at[d, shards(p)],
            r_ssend.at[d, p], r_srecv.at[d, p], me, sib,
        )

    def rs_y(d, p):
        return remote(
            y_send.at[d, shards(p)], y_recv.at[d, shards(p)],
            r_ysend.at[d, p], r_yrecv.at[d, p], me, lax.rem(mf + 2 * d, nf),
        )

    def queries_of(f):
        for i in range(rows_dev // BLK):
            attend(f * (rows_dev // BLK) + i)

    def share(f, dst, d, p):
        grad = gq[pl.ds(pl.multiple_of(f * rows_dev, rows_dev), rows_dev), :]

        @pl.loop(p * per, (p + 1) * per)
        def _(m):
            dst[d, m] = dot_nt(grad, wf[m]).astype(jnp.bfloat16)

    @pl.loop(0, ny)
    def _(i):
        d = lax.rem(i + 1, ny)
        f_sib = lax.rem(sib + 2 * d, nf)
        f_own = lax.rem(mf + 2 * d, nf)
        queries_of(f_sib)
        for p in range(parts):
            share(f_sib, p_send, d, p)
            rs_s(d, p).start()
        queries_of(f_own)
        for p in range(parts):
            share(f_own, p_own, d, p)
            rs_s(d, p).wait_recv()

            @pl.when(d > 0)
            def _():
                for m in range(p * per, (p + 1) * per):
                    y_send[d, m] = (
                        p_own[d, m].astype(jnp.float32) + s_recv[d, m].astype(jnp.float32)
                    ).astype(jnp.bfloat16)
                rs_y(d, p).start()

    for p in range(parts):
        for d in range(1, ny):
            rs_y(d, p).wait_recv()
    for m in range(n):
        total = p_own[0, m].astype(jnp.float32) + s_recv[0, m].astype(jnp.float32)
        for d in range(1, ny):
            total = total + y_recv[d, m].astype(jnp.float32)
        gin_ref[:, m * dk:(m + 1) * dk] = total.astype(jnp.bfloat16)

    @pl.loop(1, n)
    def _(d):
        peer = lax.rem(me + d, n)
        id_copy(peer, me).wait_send()
        block_copy(peer, me).wait_send()

    for zz in range(nz):
        @pl.when((zz <= z) & (z + 1 < nz))
        def _():
            w_up_copy(zz).wait_send()

        @pl.when((zz >= z) & (z > 0))
        def _():
            w_down_copy(zz).wait_send()

        for r in range(nx - 1):
            w_x_copy(r, zz).wait_send()
    for d in range(ny):
        if d:
            x_ycopy(d).wait_send()
        x_scopy(lax.rem(mf + 2 * d, nf)).wait_send()
        for p in range(parts):
            rs_s(d, p).wait_send()
            if d:
                rs_y(d, p).wait_send()


def local(n, nf, layer_input, w_query, local_kv, memory_kv, memory_ids, grad_out):
    nx = 2 ** ((n.bit_length() - 1) // 2)
    nz = n // nx
    ny = nf // 2
    rows_dev, d_model = layer_input.shape
    dk, width = w_query.shape
    ctx = rows_dev * nf
    tiles, topk = memory_ids.shape
    mb_dev = memory_kv.shape[0]
    flat = memory_ids.reshape(1, tiles * topk)
    ids_v = jnp.pad(flat, ((0, 7), (0, 128 - tiles * topk)))
    bf, f32, i32 = jnp.bfloat16, jnp.float32, jnp.int32
    any_spec = pl.BlockSpec(memory_space=pl.ANY)
    vmem_spec = pl.BlockSpec(memory_space=pltpu.VMEM)
    dma = pltpu.SemaphoreType.DMA
    heads = width // HD
    pre = 2 * heads * ctx * ctx * 4 <= 12 * 1024 * 1024
    parts = math.gcd(n, 4)
    loc_grid = pltpu.VMEM((heads, ctx, ctx) if pre else (8, 128), f32)
    part = pltpu.VMEM((ny, n, rows_dev, dk), bf)
    return pl.pallas_call(
        functools.partial(kernel, n, nx, nf, topk, mb_dev, pre, parts),
        out_shape=(
            jax.ShapeDtypeStruct((ctx, width), bf),
            jax.ShapeDtypeStruct((rows_dev, d_model), bf),
        ),
        in_specs=[pl.BlockSpec(memory_space=pltpu.SMEM), vmem_spec] + [any_spec] * 5,
        out_specs=(vmem_spec, vmem_spec),
        scratch_shapes=[
            pltpu.VMEM((n, dk, width), bf),
            pltpu.VMEM((ctx, d_model), bf),
            pltpu.VMEM(memory_kv.shape, bf),
            pltpu.VMEM(local_kv.shape, bf),
            pltpu.VMEM(grad_out.shape, bf),
            pltpu.VMEM((n,) + memory_kv.shape[1:], bf),
            pltpu.VMEM((n, 8, 128), i32),
            pltpu.VMEM((n,) + memory_kv.shape[1:], bf),
            pltpu.SMEM((n, 8, 128), i32),
            pltpu.VMEM((ctx, width), f32),
            pltpu.VMEM((ctx, width), bf),
            pltpu.VMEM((ctx, width), bf),
            part, part, part, part, part, loc_grid, loc_grid,
            dma((5,)), dma((n,)), dma((n,)), dma((1,)),
            dma((nz,)), dma((nz,)), dma((max(nx - 1, 1), nz)), dma((nz,)),
            dma((max(nx - 1, 1), nz)),
            dma((ny,)), dma((nf,)), dma((nf,)), dma((n,)), dma((n,)),
            dma((ny, parts)), dma((ny, parts)), dma((ny, parts)), dma((ny, parts)),
        ],
        compiler_params=pltpu.CompilerParams(
            collective_id=0, has_side_effects=True, vmem_limit_bytes=62 * 1024 * 1024
        ),
    )(memory_ids, ids_v, layer_input, w_query, local_kv, memory_kv, grad_out)


def solution(mesh):
    placed = (
        P(("mem", "fsdp"), None),
        P("mem", "fsdp"),
        P(None, "mem", "fsdp"),
        P("mem", None, None, "fsdp"),
        P("mem", None),
        P("mem", "fsdp"),
    )
    return jax.shard_map(
        functools.partial(local, mesh.shape["mem"], mesh.shape["fsdp"]),
        mesh=mesh,
        in_specs=placed,
        out_specs=(P("mem", "fsdp"), P(("mem", "fsdp"), None)),
        check_vma=False,
    )
```

profile of v0, /device:TPU:0, one launch (start us, length us, event | category | flops | bytes accessed | tf_op | source)
XLA Modules:
  0.0 119.2 jit_solution(10023623253128461580)
XLA Ops:
  0.6 0.8 reshape.7
  1.4 0.6 pad.4.ids_v
  2.0 113.1 %shard_map.77 = (bf16[512,512]{1,0:T(8,128)(2,1)}, bf16[128,4096]{1,0:T(8,128)(2,1)}) custom-call(s32[4,4]{1,0:T(4,128)} %ids_s.1, s32[8,128]{1,0:T(8,128)} %pad.4.ids_v, bf16[128,4096]{1,0:T(8,128)(2,1)} %x_hbm.1, bf16[512,512]{1,0:T(8,128)(2,1)} %w_hbm.1, bf16[2,512,512]{2,1,0:T(8,128)(2,1)} %lkv_hbm.1, bf16[16,2,128,512]{3,2,1,0:T(8,128)(2,1)} %mkv_hbm.1, ...), custom_call_target="tpu_custom_call" | custom-call | tf_op jit(solution)/shard_map/pallas_call | solution.py:411
  115.1 1.9 %copy.10 = bf16[512,512]{1,0:T(8,128)(2,1)} copy(bf16[512,512]{1,0:T(8,128)(2,1)} %get-tuple-element.4) | data formatting | bytes 1048576
  116.9 2.3 %copy.11 = bf16[128,4096]{1,0:T(8,128)(2,1)} copy(bf16[128,4096]{1,0:T(8,128)(2,1)} %get-tuple-element.5) | data formatting | bytes 2097152
where the time goes:
time: 119 us
  Pallas kernels  113 us (95%)
  local copies, waits for them, and re-layouts  5.52 us (5%)
    pallas_call x1, Pallas kernels, local(): pl.pallas_call(functools.partial(kernel, n, nx, nf, topk, mb_dev, pre, pa...  113 us
    unnamed x2, local copies, waits for them, and re-layouts  4.16 us

commit v1 on v0

v1 whole, which is shorter than its diff:
```python
import functools
import math

import jax
import jax.numpy as jnp
from jax import lax
from jax.experimental import pallas as pl
from jax.experimental.pallas import tpu as pltpu
from jax.sharding import PartitionSpec as P

HD = 128
BLK = 128
NEG_FILL = -1e30
MESH = pl.DeviceIdType.MESH
NT = (((1,), (1,)), ((), ()))


def dot_nn(a, b):
    return jnp.dot(a, b, preferred_element_type=jnp.float32)


def dot_nt(a, b):
    return lax.dot_general(a, b, NT, preferred_element_type=jnp.float32)


def kernel(
    n, nx, nf, mb_dev, early, per,
    ids_s, ids_v, x_hbm, w_hbm, lkv_hbm, mkv_hbm, go_hbm,
    att_ref, gin_ref,
    wf, xf, kv, lkv, go, outbox, inbox, stage, ids_in, ids_sm, q32, qb, gq,
    part, s_recv, y_send, y_recv, wy, gq_in,
    l_sem, i_send, i_recv, i_loc, w_up, w_down, w_x, w_recv, wx_recv,
    x_ysend, x_ssend, x_recv, m_send, m_recv, r_ssend, r_srecv, r_ysend, r_yrecv,
    v_ysend, v_ssend, v_recv, g_send, g_recv,
):
    me = lax.axis_index("mem")
    mf = lax.axis_index("fsdp")
    nz = n // nx
    z, xx = me // nx, lax.rem(me, nx)
    ny = nf // 2
    yy, cc = mf // 2, lax.rem(mf, 2)
    sib = mf + 1 - 2 * cc
    dk = wf.shape[1]
    width = wf.shape[2]
    heads = width // HD
    tiles, topk = ids_s.shape
    rows_dev = xf.shape[0] // nf
    late = early * HD

    def local_copy(src, dst, k):
        return pltpu.make_async_copy(src, dst, l_sem.at[k])

    def rows_of(f):
        return pl.ds(pl.multiple_of(f * rows_dev, rows_dev), rows_dev)

    c_w = local_copy(w_hbm, wf.at[me], 0)
    c_x = local_copy(x_hbm, xf.at[rows_of(mf), :], 1)
    c_kv = local_copy(mkv_hbm, kv, 2)
    c_lkv = local_copy(lkv_hbm, lkv, 3)
    c_go = local_copy(go_hbm, go, 4)
    c_w.start()
    c_x.start()
    c_kv.start()
    c_lkv.start()
    c_go.start()

    barrier = pltpu.get_barrier_semaphore()

    @pl.loop(1, n)
    def _(d):
        pl.semaphore_signal(
            barrier, inc=1, device_id=(lax.rem(me + d, n), mf), device_id_type=MESH
        )

    for d in range(1, nf):
        pl.semaphore_signal(
            barrier, inc=1, device_id=(me, lax.rem(mf + d, nf)), device_id_type=MESH
        )
    pl.semaphore_wait(barrier, n - 1 + nf - 1)

    def remote(src, dst, s, r, dm, df):
        return pltpu.make_async_remote_copy(
            src_ref=src, dst_ref=dst, send_sem=s, recv_sem=r,
            device_id=(dm, df), device_id_type=MESH,
        )

    def id_copy(peer, slot):
        return remote(ids_v, inbox.at[slot], i_send.at[peer], i_recv.at[slot], peer, mf)

    @pl.loop(1, n)
    def _(d):
        id_copy(lax.rem(me + d, n), me).start()

    def w_copy(slot, sem, dst_m, rsem):
        return remote(wf.at[slot], wf.at[slot], sem, rsem, dst_m, mf)

    def w_up_copy(zz):
        return w_copy(zz * nx + xx, w_up.at[zz], me + nx, w_recv.at[zz])

    def w_down_copy(zz):
        return w_copy(zz * nx + xx, w_down.at[zz], me - nx, w_recv.at[zz])

    x_next = z * nx + lax.rem(xx + 1, nx)

    def w_x_copy(r, zz):
        slot = zz * nx + lax.rem(xx - r + nx, nx)
        return w_copy(slot, w_x.at[r, zz], x_next, wx_recv.at[r, zz])

    def w_x_arrival(r, zz):
        slot = zz * nx + lax.rem(xx - 1 - r + 2 * nx, nx)
        return w_copy(slot, w_x.at[r, zz], x_next, wx_recv.at[r, zz])

    late_cols = slice(late, width)

    def v_ycopy(d, zz):
        return remote(
            wf.at[zz * nx + xx, :, late_cols], wy.at[mf, zz],
            v_ysend.at[d, zz], v_recv.at[mf, zz], me, lax.rem(mf + 2 * d, nf),
        )

    def v_own(zz):
        return remote(
            wf.at[zz * nx + xx, :, late_cols], wy.at[mf, zz],
            v_ssend.at[mf, zz], v_recv.at[mf, zz], me, sib,
        )

    def v_fwd(f, zz):
        return remote(
            wy.at[f, zz], wy.at[f, zz], v_ssend.at[f, zz], v_recv.at[f, zz], me, sib
        )

    def v_start(zz):
        for d in range(1, ny):
            v_ycopy(d, zz).start()
        v_own(zz).start()

    c_w.wait()

    @pl.when(z + 1 < nz)
    def _():
        w_up_copy(z).start()

    @pl.when(z > 0)
    def _():
        w_down_copy(z).start()

    w_x_copy(0, z).start()
    c_x.wait()

    def x_ycopy(d):
        return remote(
            xf.at[rows_of(mf), :], xf.at[rows_of(mf), :], x_ysend.at[d], x_recv.at[mf],
            me, lax.rem(mf + 2 * d, nf),
        )

    def x_scopy(f):
        return remote(
            xf.at[rows_of(f), :], xf.at[rows_of(f), :], x_ssend.at[f], x_recv.at[f], me, sib
        )

    for d in range(1, ny):
        x_ycopy(d).start()
    x_scopy(mf).start()
    v_start(z)

    @pl.loop(1, n)
    def _(d):
        src = lax.rem(me + d, n)
        id_copy(src, src).wait_recv()

    c_ids = pltpu.make_async_copy(inbox, ids_sm, i_loc.at[0])
    c_ids.start()
    c_kv.wait()
    c_ids.wait()

    def head_slice(h):
        return slice(h * HD, (h + 1) * HD)

    @pl.loop(1, n)
    def _(d):
        peer = lax.rem(me + d, n)
        want = jnp.int32(0)
        for j in range(tiles * topk):
            one = ids_sm[peer, j // topk, j % topk]
            want = jnp.where(one // mb_dev == me, lax.rem(one, mb_dev), want)
        for h in range(heads):
            outbox[peer, h] = kv[want, :, :, head_slice(h)]

    mine = jnp.int32(0)
    for j in range(tiles * topk):
        one = ids_s[j // topk, j % topk]
        mine = jnp.where(one // mb_dev == me, lax.rem(one, mb_dev), mine)
    for h in range(heads):
        ids_in[me, h] = kv[mine, :, :, head_slice(h)]

    def block_copy(peer, slot, h):
        return remote(
            outbox.at[peer, h], ids_in.at[slot, h], m_send.at[peer, h], m_recv.at[slot, h],
            peer, mf,
        )

    def send_blocks(hs, wanted):
        for h in hs:
            @pl.loop(1, n)
            def _(d):
                peer = lax.rem(me + n - d, n)

                @pl.when(wanted(peer // nx, lax.rem(peer, nx)))
                def _():
                    block_copy(peer, me, h).start()

    def inner(pz):
        return (pz > 0) & (pz < nz - 1)

    for k in range(1, nz):
        @pl.when(z - k >= 0)
        def _():
            w_up_copy(z - k).wait_recv()

            @pl.when(z + 1 < nz)
            def _():
                w_up_copy(z - k).start()

            w_x_copy(0, z - k).start()
            v_start(z - k)

        @pl.when(z + k < nz)
        def _():
            w_down_copy(z + k).wait_recv()

            @pl.when(z > 0)
            def _():
                w_down_copy(z + k).start()

            w_x_copy(0, z + k).start()
            v_start(z + k)

        if k == min(2, nz - 1):
            send_blocks(range(heads), lambda pz, px: (px == xx) & inner(pz))
            for d in range(1, ny):
                f = lax.rem(mf + 2 * d, nf)
                x_scopy(f).wait_recv()
                x_scopy(f).start()

    send_blocks(range(heads), lambda pz, px: (px == xx) & jnp.logical_not(inner(pz)))
    send_blocks(range(heads), lambda pz, px: px != xx)

    for d in range(ny):
        x_scopy(lax.rem(sib + 2 * d, nf)).wait_recv()

    q32[...] = jnp.zeros_like(q32)

    def project(slot):
        q32[...] += dot_nn(xf[:, pl.ds(pl.multiple_of(slot * dk, dk), dk)], wf[slot])

    def by_distance(body):
        body(z)
        for k in range(1, nz):
            for zz in (z - k, z + k):
                @pl.when((zz >= 0) & (zz < nz))
                def _():
                    body(zz)

    @pl.loop(0, nz)
    def _(zz):
        project(zz * nx + xx)

    for r in range(nx - 1):
        def arrived(zz):
            w_x_arrival(r, zz).wait_recv()
            if r + 1 < nx - 1:
                w_x_copy(r + 1, zz).start()
            project(zz * nx + lax.rem(xx - 1 - r + 2 * nx, nx))

        by_distance(arrived)

    qb[...] = q32[...].astype(jnp.bfloat16)
    c_lkv.wait()
    c_go.wait()

    scale = 1.0 / math.sqrt(HD)
    rate = scale * math.log2(math.e)
    causal = lax.broadcasted_iota(jnp.int32, (BLK, BLK), 0) >= (
        lax.broadcasted_iota(jnp.int32, (BLK, BLK), 1)
    )

    def attend(h):
        cols = pl.ds(pl.multiple_of(h * HD, HD), HD)

        @pl.loop(1, n)
        def _(d):
            src = lax.rem(me + d, n)
            block_copy(src, src, h).wait_recv()

        stage[...] = ids_in[:, h]
        for t in range(tiles):
            rows = slice(t * BLK, (t + 1) * BLK)
            span = (t + 1) * BLK
            owners = [ids_s[t, j] // mb_dev for j in range(topk)]
            keys = jnp.concatenate(
                [stage[o, 0] for o in owners] + [lkv[0, 0:span, cols]], axis=0
            )
            vals = jnp.concatenate(
                [stage[o, 1] for o in owners] + [lkv[1, 0:span, cols]], axis=0
            )
            s = dot_nt(qb[rows, cols], keys)
            dp = dot_nt(go[rows, cols], vals)
            edge = s.shape[1] - BLK
            s = jnp.concatenate(
                [s[:, :edge], jnp.where(causal, s[:, edge:], NEG_FILL)], axis=1
            )
            top = jnp.max(s, axis=1, keepdims=True)
            e = jnp.exp2((s - top) * rate)
            inv = 1.0 / jnp.sum(e, axis=1, keepdims=True)
            att_ref[rows, cols] = (dot_nn(e.astype(jnp.bfloat16), vals) * inv).astype(
                jnp.bfloat16
            )
            delta = jnp.sum(e * dp, axis=1, keepdims=True) * inv
            ds = (e * (dp - delta)).astype(jnp.bfloat16)
            gq[rows, cols] = (dot_nn(ds, keys) * (inv * scale)).astype(jnp.bfloat16)

    groups = n // per
    near = nz // per

    def slot_of(p):
        return lax.rem(p, nz) * nx + lax.rem(xx + p // nz, nx)

    def span_of(g):
        return pl.ds(g * per, per)

    own_half = pl.ds(pl.multiple_of(cc * rows_dev, rows_dev), rows_dev)
    sib_half = pl.ds(pl.multiple_of((1 - cc) * rows_dev, rows_dev), rows_dev)

    def rs_s(d, g):
        return remote(
            part.at[d, span_of(g), sib_half, :], s_recv.at[d, span_of(g)],
            r_ssend.at[d, g], r_srecv.at[d, g], me, sib,
        )

    def rs_y(d, g):
        return remote(
            y_send.at[d, span_of(g)], y_recv.at[d, span_of(g)],
            r_ysend.at[d, g], r_yrecv.at[d, g], me, lax.rem(mf + 2 * d, nf),
        )

    def shares(first, last, cols):
        for d in list(range(1, ny)) + [0]:
            chip = lax.rem(yy + d, ny)
            rows = pl.ds(pl.multiple_of(chip * 2 * rows_dev, 2 * rows_dev), 2 * rows_dev)

            @pl.loop(first, last)
            def _(g):
                for i in range(per):
                    p = g * per + i
                    part[d, p] = dot_nt(gq[rows, cols], wf[slot_of(p), :, cols]).astype(
                        jnp.bfloat16
                    )
                rs_s(d, g).start()

        for d in range(1, ny):
            @pl.loop(first, last)
            def _(g):
                rs_s(d, g).wait_recv()
                for i in range(per):
                    p = g * per + i
                    y_send[d, p] = (
                        part[d, p, own_half, :].astype(jnp.float32)
                        + s_recv[d, p].astype(jnp.float32)
                    ).astype(jnp.bfloat16)
                rs_y(d, g).start()

    def settled(p):
        total = part[0, p, own_half, :].astype(jnp.float32) + s_recv[0, p].astype(jnp.float32)
        for d in range(1, ny):
            total = total + y_recv[d, p].astype(jnp.float32)
        return total

    def g_copy(f, src):
        return remote(
            gq.at[rows_of(f), late_cols], gq_in.at[src], g_send.at[f], g_recv.at[src], me, f
        )

    @pl.loop(0, early)
    def _(h):
        attend(h)

    shares(0, near, slice(0, late))

    for d in range(1, ny):
        f = lax.rem(mf + 2 * d, nf)

        @pl.loop(0, nz)
        def _(zz):
            v_fwd(f, zz).wait_recv()
            v_fwd(f, zz).start()

    @pl.loop(early, heads)
    def _(h):
        attend(h)

    for d in range(1, nf):
        g_copy(lax.rem(mf + d, nf), mf).start()

    shares(near, groups, slice(0, width))

    for d in range(ny):
        f = lax.rem(sib + 2 * d, nf)

        @pl.loop(0, nz)
        def _(zz):
            v_fwd(f, zz).wait_recv()

    for d in range(1, nf):
        f = lax.rem(mf + d, nf)
        g_copy(f, f).wait_recv()

    def finish(g):
        rs_s(0, g).wait_recv()
        for d in range(1, ny):
            rs_y(d, g).wait_recv()

    def out_cols(p):
        return pl.ds(pl.multiple_of(slot_of(p) * dk, dk), dk)

    @pl.loop(0, near)
    def _(g):
        finish(g)
        for i in range(per):
            p = g * per + i
            total = settled(p) + dot_nt(gq[rows_of(mf), late_cols], wf[slot_of(p), :, late_cols])
            for d in range(1, nf):
                f = lax.rem(mf + d, nf)
                total = total + dot_nt(gq_in[f], wy[f, p])
            gin_ref[:, out_cols(p)] = total.astype(jnp.bfloat16)

    @pl.loop(near, groups)
    def _(g):
        finish(g)
        for i in range(per):
            p = g * per + i
            gin_ref[:, out_cols(p)] = settled(p).astype(jnp.bfloat16)

    @pl.loop(1, n)
    def _(d):
        peer = lax.rem(me + d, n)
        id_copy(peer, me).wait_send()
        for h in range(heads):
            block_copy(peer, me, h).wait_send()

    @pl.loop(0, nz)
    def _(zz):
        @pl.when((zz <= z) & (z + 1 < nz))
        def _():
            w_up_copy(zz).wait_send()

        @pl.when((zz >= z) & (z > 0))
        def _():
            w_down_copy(zz).wait_send()

        for r in range(nx - 1):
            w_x_copy(r, zz).wait_send()
        for d in range(1, ny):
            v_ycopy(d, zz).wait_send()
            v_fwd(lax.rem(mf + 2 * d, nf), zz).wait_send()
        v_own(zz).wait_send()

    for d in range(ny):
        if d:
            x_ycopy(d).wait_send()
        x_scopy(lax.rem(mf + 2 * d, nf)).wait_send()

        @pl.loop(0, groups)
        def _(g):
            rs_s(d, g).wait_send()
            if d:
                rs_y(d, g).wait_send()

    for d in range(1, nf):
        g_copy(lax.rem(mf + d, nf), mf).wait_send()


def emit(a_ref, b_ref, c_ref, d_ref):
    c_ref[...] = a_ref[...]
    d_ref[...] = b_ref[...]


def local(n, nf, layer_input, w_query, local_kv, memory_kv, memory_ids, grad_out):
    nx = 2 ** ((n.bit_length() - 1) // 2)
    nz = n // nx
    ny = nf // 2
    rows_dev, d_model = layer_input.shape
    dk, width = w_query.shape
    ctx = rows_dev * nf
    mb_dev = memory_kv.shape[0]
    bf, f32, i32 = jnp.bfloat16, jnp.float32, jnp.int32
    any_spec = pl.BlockSpec(memory_space=pl.ANY)
    vmem_spec = pl.BlockSpec(memory_space=pltpu.VMEM)
    dma = pltpu.SemaphoreType.DMA
    heads = width // HD
    early = heads // 2
    lw = width - early * HD
    per = max(1, nz // 4)
    groups = n // per
    blocks = pltpu.VMEM((n, heads, 2, BLK, HD), bf)
    piece = pltpu.VMEM((ny, n, rows_dev, dk), bf)
    outs = (
        jax.ShapeDtypeStruct((ctx, width), bf),
        jax.ShapeDtypeStruct((rows_dev, d_model), bf),
    )
    raw = pl.pallas_call(
        functools.partial(kernel, n, nx, nf, mb_dev, early, per),
        out_shape=outs,
        in_specs=[pl.BlockSpec(memory_space=pltpu.SMEM), vmem_spec] + [any_spec] * 5,
        out_specs=(vmem_spec, vmem_spec),
        scratch_shapes=[
            pltpu.VMEM((n, dk, width), bf),
            pltpu.VMEM((ctx, d_model), bf),
            pltpu.VMEM(memory_kv.shape, bf),
            pltpu.VMEM(local_kv.shape, bf),
            pltpu.VMEM(grad_out.shape, bf),
            blocks,
            pltpu.VMEM((n,) + memory_ids.shape, i32),
            pltpu.VMEM((n, 2, BLK, HD), bf),
            blocks,
            pltpu.SMEM((n,) + memory_ids.shape, i32),
            pltpu.VMEM((ctx, width), f32),
            pltpu.VMEM((ctx, width), bf),
            pltpu.VMEM((ctx, width), bf),
            pltpu.VMEM((ny, n, 2 * rows_dev, dk), bf), piece, piece, piece,
            pltpu.VMEM((nf, nz, dk, lw), bf),
            pltpu.VMEM((nf, rows_dev, lw), bf),
            dma((5,)), dma((n,)), dma((n,)), dma((1,)),
            dma((nz,)), dma((nz,)), dma((max(nx - 1, 1), nz)), dma((nz,)),
            dma((max(nx - 1, 1), nz)),
            dma((ny,)), dma((nf,)), dma((nf,)), dma((n, heads)), dma((n, heads)),
            dma((ny, groups)), dma((ny, groups)), dma((ny, groups)), dma((ny, groups)),
            dma((ny, nz)), dma((nf, nz)), dma((nf, nz)), dma((nf,)), dma((nf,)),
        ],
        compiler_params=pltpu.CompilerParams(
            collective_id=0, has_side_effects=True, vmem_limit_bytes=62 * 1024 * 1024
        ),
    )(memory_ids, memory_ids, layer_input, w_query, local_kv, memory_kv, grad_out)
    return pl.pallas_call(emit, out_shape=outs)(*raw)


def solution(mesh):
    placed = (
        P(("mem", "fsdp"), None),
        P("mem", "fsdp"),
        P(None, "mem", "fsdp"),
        P("mem", None, None, "fsdp"),
        P("mem", None),
        P("mem", "fsdp"),
    )
    return jax.shard_map(
        functools.partial(local, mesh.shape["mem"], mesh.shape["fsdp"]),
        mesh=mesh,
        in_specs=placed,
        out_specs=(P("mem", "fsdp"), P(("mem", "fsdp"), None)),
        check_vma=False,
    )
```

time: 119 us -> 119 us (level)
  local copies, waits for them, and re-layouts: 5.52 us -> 0 us
  Pallas kernels: 113 us -> 118 us
    pallas_call x1 -> x2, Pallas kernels: 113 us -> 118 us  [the longest x1 116 us: local(): pl.pallas_call(functools.partial(kernel, n, nx, nf, mb_dev, early, per),...]
    unnamed x2 -> x0, local copies, waits for them, and re-layouts: 4.16 us -> none
where the time goes in v1:
time: 119 us
  Pallas kernels  118 us (99%)
    pallas_call x1, Pallas kernels, local(): pl.pallas_call(functools.partial(kernel, n, nx, nf, mb_dev, early, per),...  116 us
    pallas_call x1, Pallas kernels, local(): return pl.pallas_call(emit, out_shape=outs)(*raw)  2.57 us

profile of v1, /device:TPU:0, one launch (start us, length us, event | category | flops | bytes accessed | tf_op | source)
XLA Modules:
  0.0 118.8 jit_solution(3087362181969599910)
XLA Ops:
  0.6 115.6 %shard_map.77 = (bf16[512,512]{1,0:T(8,128)(2,1)}, bf16[128,4096]{1,0:T(8,128)(2,1)}) custom-call(s32[4,4]{1,0:T(4,128)} %ids_v.1, s32[4,4]{1,0:T(4,128)} %ids_v.1, bf16[128,4096]{1,0:T(8,128)(2,1)} %x_hbm.1, bf16[512,512]{1,0:T(8,128)(2,1)} %w_hbm.1, bf16[2,512,512]{2,1,0:T(8,128)(2,1)} %lkv_hbm.1, bf16[16,2,128,512]{3,2,1,0:T(8,128)(2,1)} %mkv_hbm.1, ...), custom_call_target="tpu_custom_call" | custom-call | tf_op jit(solution)/shard_map/pallas_call | solution.py:510
  116.2 2.6 %shard_map.78 = (bf16[512,512]{1,0:T(8,128)(2,1)}, bf16[128,4096]{1,0:T(8,128)(2,1)}) custom-call(bf16[512,512]{1,0:T(8,128)(2,1)} %get-tuple-element.4.a_ref, bf16[128,4096]{1,0:T(8,128)(2,1)} %get-tuple-element.5.b_ref), custom_call_target="tpu_custom_call" | custom-call | tf_op jit(solution)/shard_map/pallas_call | solution.py:543

commit v2 on v1

--- a/solution.py
+++ b/solution.py
@@ -24,7 +24,7 @@
 
 
 def kernel(
-    n, nx, nf, mb_dev, early, per,
+    n, nx, nf, mb_dev, early, per, full, swap,
     ids_s, ids_v, x_hbm, w_hbm, lkv_hbm, mkv_hbm, go_hbm,
     att_ref, gin_ref,
     wf, xf, kv, lkv, go, outbox, inbox, stage, ids_in, ids_sm, q32, qb, gq,
@@ -46,6 +46,8 @@
     tiles, topk = ids_s.shape
     rows_dev = xf.shape[0] // nf
     late = early * HD
+    late_cols = slice(late, width)
+    halves = (slice(0, late), late_cols)
 
     def local_copy(src, dst, k):
         return pltpu.make_async_copy(src, dst, l_sem.at[k])
@@ -91,60 +93,67 @@
     def _(d):
         id_copy(lax.rem(me + d, n), me).start()
 
-    def w_copy(slot, sem, dst_m, rsem):
-        return remote(wf.at[slot], wf.at[slot], sem, rsem, dst_m, mf)
-
-    def w_up_copy(zz):
-        return w_copy(zz * nx + xx, w_up.at[zz], me + nx, w_recv.at[zz])
-
-    def w_down_copy(zz):
-        return w_copy(zz * nx + xx, w_down.at[zz], me - nx, w_recv.at[zz])
+    def w_copy(slot, c, sem, dst_m, rsem):
+        piece = wf.at[slot, :, halves[c]]
+        return remote(piece, piece, sem, rsem, dst_m, mf)
+
+    def w_up_copy(zz, c):
+        return w_copy(zz * nx + xx, c, w_up.at[zz, c], me + nx, w_recv.at[zz, c])
+
+    def w_down_copy(zz, c):
+        return w_copy(zz * nx + xx, c, w_down.at[zz, c], me - nx, w_recv.at[zz, c])
 
     x_next = z * nx + lax.rem(xx + 1, nx)
 
-    def w_x_copy(r, zz):
+    def w_x_copy(r, zz, c):
         slot = zz * nx + lax.rem(xx - r + nx, nx)
-        return w_copy(slot, w_x.at[r, zz], x_next, wx_recv.at[r, zz])
-
-    def w_x_arrival(r, zz):
+        return w_copy(slot, c, w_x.at[r, zz, c], x_next, wx_recv.at[r, zz, c])
+
+    def w_x_arrival(r, zz, c):
         slot = zz * nx + lax.rem(xx - 1 - r + 2 * nx, nx)
-        return w_copy(slot, w_x.at[r, zz], x_next, wx_recv.at[r, zz])
-
-    late_cols = slice(late, width)
-
-    def v_ycopy(d, zz):
+        return w_copy(slot, c, w_x.at[r, zz, c], x_next, wx_recv.at[r, zz, c])
+
+    def slot_of(p):
+        return lax.rem(p + z, nz) * nx + lax.rem(xx - p // nz + nx, nx)
+
+    def v_halves(p):
+        return (1, 0) if p < full else (1,)
+
+    def v_first(p, c, s, df):
         return remote(
-            wf.at[zz * nx + xx, :, late_cols], wy.at[mf, zz],
-            v_ysend.at[d, zz], v_recv.at[mf, zz], me, lax.rem(mf + 2 * d, nf),
-        )
-
-    def v_own(zz):
-        return remote(
-            wf.at[zz * nx + xx, :, late_cols], wy.at[mf, zz],
-            v_ssend.at[mf, zz], v_recv.at[mf, zz], me, sib,
-        )
-
-    def v_fwd(f, zz):
-        return remote(
-            wy.at[f, zz], wy.at[f, zz], v_ssend.at[f, zz], v_recv.at[f, zz], me, sib
-        )
-
-    def v_start(zz):
-        for d in range(1, ny):
-            v_ycopy(d, zz).start()
-        v_own(zz).start()
+            wf.at[slot_of(p), :, halves[c]], wy.at[mf, p, :, halves[c]],
+            s, v_recv.at[mf, p, c], me, df,
+        )
+
+    def v_ycopy(d, p, c):
+        return v_first(p, c, v_ysend.at[d, p, c], lax.rem(mf + 2 * d, nf))
+
+    def v_own(p, c):
+        return v_first(p, c, v_ssend.at[mf, p, c], sib)
+
+    def v_fwd(f, p, c):
+        piece = wy.at[f, p, :, halves[c]]
+        return remote(piece, piece, v_ssend.at[f, p, c], v_recv.at[f, p, c], me, sib)
+
+    def v_start(p):
+        if p < swap:
+            for c in v_halves(p):
+                for d in range(1, ny):
+                    v_ycopy(d, p, c).start()
+                v_own(p, c).start()
 
     c_w.wait()
 
-    @pl.when(z + 1 < nz)
-    def _():
-        w_up_copy(z).start()
-
-    @pl.when(z > 0)
-    def _():
-        w_down_copy(z).start()
-
-    w_x_copy(0, z).start()
+    for c in range(2):
+        @pl.when(z + 1 < nz)
+        def _():
+            w_up_copy(z, c).start()
+
+        @pl.when(z > 0)
+        def _():
+            w_down_copy(z, c).start()
+
+        w_x_copy(0, z, c).start()
     c_x.wait()
 
     def x_ycopy(d):
@@ -161,7 +170,7 @@
     for d in range(1, ny):
         x_ycopy(d).start()
     x_scopy(mf).start()
-    v_start(z)
+    v_start(0)
 
     @pl.loop(1, n)
     def _(d):
@@ -209,31 +218,37 @@
                 def _():
                     block_copy(peer, me, h).start()
 
+    def send_crossing(h):
+        send_blocks((h,), lambda pz, px: px != xx)
+
     def inner(pz):
         return (pz > 0) & (pz < nz - 1)
 
     for k in range(1, nz):
-        @pl.when(z - k >= 0)
-        def _():
-            w_up_copy(z - k).wait_recv()
-
-            @pl.when(z + 1 < nz)
+        for c in range(2):
+            @pl.when(z - k >= 0)
             def _():
-                w_up_copy(z - k).start()
-
-            w_x_copy(0, z - k).start()
-            v_start(z - k)
-
-        @pl.when(z + k < nz)
-        def _():
-            w_down_copy(z + k).wait_recv()
-
-            @pl.when(z > 0)
+                w_up_copy(z - k, c).wait_recv()
+
+                @pl.when(z + 1 < nz)
+                def _():
+                    w_up_copy(z - k, c).start()
+
+                w_x_copy(0, z - k, c).start()
+                if c:
+                    v_start(nz - k)
+
+            @pl.when(z + k < nz)
             def _():
-                w_down_copy(z + k).start()
-
-            w_x_copy(0, z + k).start()
-            v_start(z + k)
+                w_down_copy(z + k, c).wait_recv()
+
+                @pl.when(z > 0)
+                def _():
+                    w_down_copy(z + k, c).start()
+
+                w_x_copy(0, z + k, c).start()
+                if c:
+                    v_start(k)
 
         if k == min(2, nz - 1):
             send_blocks(range(heads), lambda pz, px: (px == xx) & inner(pz))
@@ -242,8 +257,6 @@
                 x_scopy(f).wait_recv()
                 x_scopy(f).start()
 
-    send_blocks(range(heads), lambda pz, px: (px == xx) & jnp.logical_not(inner(pz)))
-    send_blocks(range(heads), lambda pz, px: px != xx)
 
     for d in range(ny):
         x_scopy(lax.rem(sib + 2 * d, nf)).wait_recv()
@@ -253,13 +266,18 @@
     def project(slot):
         q32[...] += dot_nn(xf[:, pl.ds(pl.multiple_of(slot * dk, dk), dk)], wf[slot])
 
-    def by_distance(body):
+    def send_outer():
+        send_blocks(range(heads), lambda pz, px: (px == xx) & jnp.logical_not(inner(pz)))
+
+    def by_distance(body, after=None):
         body(z)
         for k in range(1, nz):
             for zz in (z - k, z + k):
                 @pl.when((zz >= 0) & (zz < nz))
                 def _():
                     body(zz)
+            if after and k == 1:
+                after()
 
     @pl.loop(0, nz)
     def _(zz):
@@ -267,13 +285,19 @@
 
     for r in range(nx - 1):
         def arrived(zz):
-            w_x_arrival(r, zz).wait_recv()
-            if r + 1 < nx - 1:
-                w_x_copy(r + 1, zz).start()
+            for c in range(2):
+                w_x_arrival(r, zz, c).wait_recv()
+                if r + 1 < nx - 1:
+                    w_x_copy(r + 1, zz, c).start()
             project(zz * nx + lax.rem(xx - 1 - r + 2 * nx, nx))
 
-        by_distance(arrived)
-
+        by_distance(arrived, send_outer if r == nx - 2 else None)
+    if nx == 1:
+        send_outer()
+    for p in range(nz, swap):
+        v_start(p)
+    send_crossing(0)
+    send_crossing(1)
     qb[...] = q32[...].astype(jnp.bfloat16)
     c_lkv.wait()
     c_go.wait()
@@ -291,6 +315,10 @@
         def _(d):
             src = lax.rem(me + d, n)
             block_copy(src, src, h).wait_recv()
+
+        @pl.when(h + 2 < heads)
+        def _():
+            send_crossing(h + 2)
 
         stage[...] = ids_in[:, h]
         for t in range(tiles):
@@ -320,10 +348,6 @@
             gq[rows, cols] = (dot_nn(ds, keys) * (inv * scale)).astype(jnp.bfloat16)
 
     groups = n // per
-    near = nz // per
-
-    def slot_of(p):
-        return lax.rem(p, nz) * nx + lax.rem(xx + p // nz, nx)
 
     def span_of(g):
         return pl.ds(g * per, per)
@@ -375,44 +399,46 @@
             total = total + y_recv[d, p].astype(jnp.float32)
         return total
 
-    def g_copy(f, src):
+    def g_copy(f, src, c):
         return remote(
-            gq.at[rows_of(f), late_cols], gq_in.at[src], g_send.at[f], g_recv.at[src], me, f
-        )
+            gq.at[rows_of(f), halves[c]], gq_in.at[src, :, halves[c]],
+            g_send.at[f, c], g_recv.at[src, c], me, f,
+        )
+
+    def g_start(c):
+        for d in range(1, nf):
+            g_copy(lax.rem(mf + d, nf), mf, c).start()
 
     @pl.loop(0, early)
     def _(h):
         attend(h)
 
-    shares(0, near, slice(0, late))
-
-    for d in range(1, ny):
-        f = lax.rem(mf + 2 * d, nf)
-
-        @pl.loop(0, nz)
-        def _(zz):
-            v_fwd(f, zz).wait_recv()
-            v_fwd(f, zz).start()
+    shares(full // per, swap // per, halves[0])
+    g_start(0)
+
+    for p in range(swap):
+        for c in v_halves(p):
+            for d in range(1, ny):
+                f = lax.rem(mf + 2 * d, nf)
+                v_fwd(f, p, c).wait_recv()
+                v_fwd(f, p, c).start()
 
     @pl.loop(early, heads)
     def _(h):
         attend(h)
 
-    for d in range(1, nf):
-        g_copy(lax.rem(mf + d, nf), mf).start()
-
-    shares(near, groups, slice(0, width))
-
-    for d in range(ny):
-        f = lax.rem(sib + 2 * d, nf)
-
-        @pl.loop(0, nz)
-        def _(zz):
-            v_fwd(f, zz).wait_recv()
+    g_start(1)
+    shares(swap // per, groups, slice(0, width))
+
+    for p in range(swap):
+        for c in v_halves(p):
+            for d in range(ny):
+                v_fwd(lax.rem(sib + 2 * d, nf), p, c).wait_recv()
 
     for d in range(1, nf):
         f = lax.rem(mf + d, nf)
-        g_copy(f, f).wait_recv()
+        for c in range(2):
+            g_copy(f, f, c).wait_recv()
 
     def finish(g):
         rs_s(0, g).wait_recv()
@@ -422,18 +448,25 @@
     def out_cols(p):
         return pl.ds(pl.multiple_of(slot_of(p) * dk, dk), dk)
 
-    @pl.loop(0, near)
+    def gathered(p, cols):
+        total = dot_nt(gq[rows_of(mf), cols], wf[slot_of(p), :, cols])
+        for d in range(1, nf):
+            f = lax.rem(mf + d, nf)
+            total = total + dot_nt(gq_in[f, :, cols], wy[f, p, :, cols])
+        return total
+
+    @pl.loop(0, full)
+    def _(p):
+        gin_ref[:, out_cols(p)] = gathered(p, slice(0, width)).astype(jnp.bfloat16)
+
+    @pl.loop(full // per, swap // per)
     def _(g):
         finish(g)
         for i in range(per):
             p = g * per + i
-            total = settled(p) + dot_nt(gq[rows_of(mf), late_cols], wf[slot_of(p), :, late_cols])
-            for d in range(1, nf):
-                f = lax.rem(mf + d, nf)
-                total = total + dot_nt(gq_in[f], wy[f, p])
-            gin_ref[:, out_cols(p)] = total.astype(jnp.bfloat16)
-
-    @pl.loop(near, groups)
+            gin_ref[:, out_cols(p)] = (settled(p) + gathered(p, late_cols)).astype(jnp.bfloat16)
+
+    @pl.loop(swap // per, groups)
     def _(g):
         finish(g)
         for i in range(per):
@@ -449,34 +482,38 @@
 
     @pl.loop(0, nz)
     def _(zz):
-        @pl.when((zz <= z) & (z + 1 < nz))
-        def _():
-            w_up_copy(zz).wait_send()
-
-        @pl.when((zz >= z) & (z > 0))
-        def _():
-            w_down_copy(zz).wait_send()
-
-        for r in range(nx - 1):
-            w_x_copy(r, zz).wait_send()
-        for d in range(1, ny):
-            v_ycopy(d, zz).wait_send()
-            v_fwd(lax.rem(mf + 2 * d, nf), zz).wait_send()
-        v_own(zz).wait_send()
+        for c in range(2):
+            @pl.when((zz <= z) & (z + 1 < nz))
+            def _():
+                w_up_copy(zz, c).wait_send()
+
+            @pl.when((zz >= z) & (z > 0))
+            def _():
+                w_down_copy(zz, c).wait_send()
+
+            for r in range(nx - 1):
+                w_x_copy(r, zz, c).wait_send()
 
     for d in range(ny):
         if d:
             x_ycopy(d).wait_send()
         x_scopy(lax.rem(mf + 2 * d, nf)).wait_send()
 
-        @pl.loop(0, groups)
+        @pl.loop(full // per, groups)
         def _(g):
             rs_s(d, g).wait_send()
             if d:
                 rs_y(d, g).wait_send()
 
+    for p in range(swap):
+        for c in v_halves(p):
+            for d in range(1, ny):
+                v_ycopy(d, p, c).wait_send()
+                v_fwd(lax.rem(mf + 2 * d, nf), p, c).wait_send()
+            v_own(p, c).wait_send()
     for d in range(1, nf):
-        g_copy(lax.rem(mf + d, nf), mf).wait_send()
+        for c in range(2):
+            g_copy(lax.rem(mf + d, nf), mf, c).wait_send()
 
 
 def emit(a_ref, b_ref, c_ref, d_ref):
@@ -498,9 +535,10 @@
     dma = pltpu.SemaphoreType.DMA
     heads = width // HD
     early = heads // 2
-    lw = width - early * HD
     per = max(1, nz // 4)
     groups = n // per
+    full = nz // 2
+    swap = min(nz + per, n)
     blocks = pltpu.VMEM((n, heads, 2, BLK, HD), bf)
     piece = pltpu.VMEM((ny, n, rows_dev, dk), bf)
     outs = (
@@ -508,7 +546,7 @@
         jax.ShapeDtypeStruct((rows_dev, d_model), bf),
     )
     raw = pl.pallas_call(
-        functools.partial(kernel, n, nx, nf, mb_dev, early, per),
+        functools.partial(kernel, n, nx, nf, mb_dev, early, per, full, swap),
         out_shape=outs,
         in_specs=[pl.BlockSpec(memory_space=pltpu.SMEM), vmem_spec] + [any_spec] * 5,
         out_specs=(vmem_spec, vmem_spec),
@@ -527,14 +565,15 @@
             pltpu.VMEM((ctx, width), bf),
             pltpu.VMEM((ctx, width), bf),
             pltpu.VMEM((ny, n, 2 * rows_dev, dk), bf), piece, piece, piece,
-            pltpu.VMEM((nf, nz, dk, lw), bf),
-            pltpu.VMEM((nf, rows_dev, lw), bf),
+            pltpu.VMEM((nf, swap, dk, width), bf),
+            pltpu.VMEM((nf, rows_dev, width), bf),
             dma((5,)), dma((n,)), dma((n,)), dma((1,)),
-            dma((nz,)), dma((nz,)), dma((max(nx - 1, 1), nz)), dma((nz,)),
-            dma((max(nx - 1, 1), nz)),
+            dma((nz, 2)), dma((nz, 2)), dma((max(nx - 1, 1), nz, 2)), dma((nz, 2)),
+            dma((max(nx - 1, 1), nz, 2)),
             dma((ny,)), dma((nf,)), dma((nf,)), dma((n, heads)), dma((n, heads)),
             dma((ny, groups)), dma((ny, groups)), dma((ny, groups)), dma((ny, groups)),
-            dma((ny, nz)), dma((nf, nz)), dma((nf, nz)), dma((nf,)), dma((nf,)),
+            dma((ny, swap, 2)), dma((nf, swap, 2)), dma((nf, swap, 2)),
+            dma((nf, 2)), dma((nf, 2)),
         ],
         compiler_params=pltpu.CompilerParams(
             collective_id=0, has_side_effects=True, vmem_limit_bytes=62 * 1024 * 1024

time: 119 us -> 107 us (0.90)
  Pallas kernels: 118 us -> 106 us
    pallas_call x1, Pallas kernels: 116 us -> 104 us  [local(): pl.pallas_call(functools.partial(kernel, n, nx, nf, mb_dev, early, per, f...]
where the time goes in v2:
time: 107 us
  Pallas kernels  106 us (99%)
    pallas_call x1, Pallas kernels, local(): pl.pallas_call(functools.partial(kernel, n, nx, nf, mb_dev, early, per, f...  104 us
    pallas_call x1, Pallas kernels, local(): return pl.pallas_call(emit, out_shape=outs)(*raw)  2.57 us

profile of v2, /device:TPU:0, one launch (start us, length us, event | category | flops | bytes accessed | tf_op | source)
XLA Modules:
  0.0 107.0 jit_solution(3831919038738666119)
XLA Ops:
  0.6 103.8 %shard_map.77 = (bf16[512,512]{1,0:T(8,128)(2,1)}, bf16[128,4096]{1,0:T(8,128)(2,1)}) custom-call(s32[4,4]{1,0:T(4,128)} %ids_v.1, s32[4,4]{1,0:T(4,128)} %ids_v.1, bf16[128,4096]{1,0:T(8,128)(2,1)} %x_hbm.1, bf16[512,512]{1,0:T(8,128)(2,1)} %w_hbm.1, bf16[2,512,512]{2,1,0:T(8,128)(2,1)} %lkv_hbm.1, bf16[16,2,128,512]{3,2,1,0:T(8,128)(2,1)} %mkv_hbm.1, ...), custom_call_target="tpu_custom_call" | custom-call | tf_op jit(solution)/shard_map/pallas_call | solution.py:548
  104.4 2.6 %shard_map.78 = (bf16[512,512]{1,0:T(8,128)(2,1)}, bf16[128,4096]{1,0:T(8,128)(2,1)}) custom-call(bf16[512,512]{1,0:T(8,128)(2,1)} %get-tuple-element.4.a_ref, bf16[128,4096]{1,0:T(8,128)(2,1)} %get-tuple-element.5.b_ref), custom_call_target="tpu_custom_call" | custom-call | tf_op jit(solution)/shard_map/pallas_call | solution.py:582

commit v3 on v2

--- a/solution.py
+++ b/solution.py
@@ -24,14 +24,14 @@
 
 
 def kernel(
-    n, nx, nf, mb_dev, early, per, full, swap,
+    n, nx, nf, mb_dev, early, per, swap,
     ids_s, ids_v, x_hbm, w_hbm, lkv_hbm, mkv_hbm, go_hbm,
     att_ref, gin_ref,
     wf, xf, kv, lkv, go, outbox, inbox, stage, ids_in, ids_sm, q32, qb, gq,
     part, s_recv, y_send, y_recv, wy, gq_in,
     l_sem, i_send, i_recv, i_loc, w_up, w_down, w_x, w_recv, wx_recv,
     x_ysend, x_ssend, x_recv, m_send, m_recv, r_ssend, r_srecv, r_ysend, r_yrecv,
-    v_ysend, v_ssend, v_recv, g_send, g_recv,
+    v_ysend, v_ssend, v_recv, g_send, g_recv, seen,
 ):
     me = lax.axis_index("mem")
     mf = lax.axis_index("fsdp")
@@ -68,17 +68,28 @@
 
     barrier = pltpu.get_barrier_semaphore()
 
-    @pl.loop(1, n)
-    def _(d):
-        pl.semaphore_signal(
-            barrier, inc=1, device_id=(lax.rem(me + d, n), mf), device_id_type=MESH
-        )
-
+    x_next = z * nx + lax.rem(xx + 1, nx)
+    x_prev = z * nx + lax.rem(xx + nx - 1, nx)
+    below, above = z > 0, z + 1 < nz
+
+    def signal(sem, dm, df):
+        pl.semaphore_signal(sem, inc=1, device_id=(dm, df), device_id_type=MESH)
+
+    @pl.when(above)
+    def _():
+        signal(barrier, me + nx, mf)
+
+    @pl.when(below)
+    def _():
+        signal(barrier, me - nx, mf)
+
+    signal(barrier, x_next, mf)
+    if nx > 2:
+        signal(barrier, x_prev, mf)
     for d in range(1, nf):
-        pl.semaphore_signal(
-            barrier, inc=1, device_id=(me, lax.rem(mf + d, nf)), device_id_type=MESH
-        )
-    pl.semaphore_wait(barrier, n - 1 + nf - 1)
+        signal(barrier, me, lax.rem(mf + d, nf))
+    line = (z + nz - 2) // (nz - 1) + (2 * nz - 3 - z) // (nz - 1)
+    pl.semaphore_wait(barrier, (1 if nx == 2 else 2) + nf - 1 + line)
 
     def remote(src, dst, s, r, dm, df):
         return pltpu.make_async_remote_copy(
@@ -89,71 +100,87 @@
     def id_copy(peer, slot):
         return remote(ids_v, inbox.at[slot], i_send.at[peer], i_recv.at[slot], peer, mf)
 
+    def w_copy(slot, c, sem, dst_m, rsem):
+        piece = wf.at[slot, :, halves[c]]
+        return remote(piece, piece, sem, rsem, dst_m, mf)
+
+    def w_up_copy(zz, c):
+        return w_copy(zz * nx + xx, c, w_up.at[zz, c], me + nx, w_recv.at[zz, c])
+
+    def w_down_copy(zz, c):
+        return w_copy(zz * nx + xx, c, w_down.at[zz, c], me - nx, w_recv.at[zz, c])
+
+    def w_x_copy(r, zz, c):
+        slot = zz * nx + lax.rem(xx - r + nx, nx)
+        return w_copy(slot, c, w_x.at[r, zz, c], x_next, wx_recv.at[r, zz, c])
+
+    def w_x_arrival(r, zz, c):
+        slot = zz * nx + lax.rem(xx - 1 - r + 2 * nx, nx)
+        return w_copy(slot, c, w_x.at[r, zz, c], x_next, wx_recv.at[r, zz, c])
+
+    turn = 1 - 2 * ((z + 1) // nz)
+
+    def slot_of(p):
+        return lax.rem(z + turn * lax.rem(p, nz) + nz, nz) * nx + lax.rem(xx - p // nz + nx, nx)
+
+    def v_first(p, s, df):
+        return remote(
+            wf.at[slot_of(p), :, late_cols], wy.at[mf, p], s, v_recv.at[mf, p], me, df
+        )
+
+    def v_ycopy(d, p):
+        return v_first(p, v_ysend.at[d, p], lax.rem(mf + 2 * d, nf))
+
+    def v_own(p):
+        return v_first(p, v_ssend.at[mf, p], sib)
+
+    def v_fwd(f, p):
+        return remote(
+            wy.at[f, p], wy.at[f, p], v_ssend.at[f, p], v_recv.at[f, p], me, sib
+        )
+
+    def v_start(p):
+        for d in range(1, ny):
+            v_ycopy(d, p).start()
+        v_own(p).start()
+
+    c_w.wait()
+
+    def w_begin(c):
+        @pl.when(above)
+        def _():
+            w_up_copy(z, c).start()
+
+        @pl.when(below)
+        def _():
+            w_down_copy(z, c).start()
+
+        w_x_copy(0, z, c).start()
+
+    w_begin(0)
+
+    @pl.when(below)
+    def _():
+        pl.semaphore_wait(seen.at[0], 1)
+
+    @pl.when(above)
+    def _():
+        signal(seen.at[0], me + nx, mf)
+        pl.semaphore_wait(seen.at[1], 1)
+
+    @pl.when(below)
+    def _():
+        signal(seen.at[1], me - nx, mf)
+
+    for r in range(nx - 1):
+        signal(seen.at[2], x_next, mf)
+        pl.semaphore_wait(seen.at[2], 1)
+
     @pl.loop(1, n)
     def _(d):
         id_copy(lax.rem(me + d, n), me).start()
 
-    def w_copy(slot, c, sem, dst_m, rsem):
-        piece = wf.at[slot, :, halves[c]]
-        return remote(piece, piece, sem, rsem, dst_m, mf)
-
-    def w_up_copy(zz, c):
-        return w_copy(zz * nx + xx, c, w_up.at[zz, c], me + nx, w_recv.at[zz, c])
-
-    def w_down_copy(zz, c):
-        return w_copy(zz * nx + xx, c, w_down.at[zz, c], me - nx, w_recv.at[zz, c])
-
-    x_next = z * nx + lax.rem(xx + 1, nx)
-
-    def w_x_copy(r, zz, c):
-        slot = zz * nx + lax.rem(xx - r + nx, nx)
-        return w_copy(slot, c, w_x.at[r, zz, c], x_next, wx_recv.at[r, zz, c])
-
-    def w_x_arrival(r, zz, c):
-        slot = zz * nx + lax.rem(xx - 1 - r + 2 * nx, nx)
-        return w_copy(slot, c, w_x.at[r, zz, c], x_next, wx_recv.at[r, zz, c])
-
-    def slot_of(p):
-        return lax.rem(p + z, nz) * nx + lax.rem(xx - p // nz + nx, nx)
-
-    def v_halves(p):
-        return (1, 0) if p < full else (1,)
-
-    def v_first(p, c, s, df):
-        return remote(
-            wf.at[slot_of(p), :, halves[c]], wy.at[mf, p, :, halves[c]],
-            s, v_recv.at[mf, p, c], me, df,
-        )
-
-    def v_ycopy(d, p, c):
-        return v_first(p, c, v_ysend.at[d, p, c], lax.rem(mf + 2 * d, nf))
-
-    def v_own(p, c):
-        return v_first(p, c, v_ssend.at[mf, p, c], sib)
-
-    def v_fwd(f, p, c):
-        piece = wy.at[f, p, :, halves[c]]
-        return remote(piece, piece, v_ssend.at[f, p, c], v_recv.at[f, p, c], me, sib)
-
-    def v_start(p):
-        if p < swap:
-            for c in v_halves(p):
-                for d in range(1, ny):
-                    v_ycopy(d, p, c).start()
-                v_own(p, c).start()
-
-    c_w.wait()
-
-    for c in range(2):
-        @pl.when(z + 1 < nz)
-        def _():
-            w_up_copy(z, c).start()
-
-        @pl.when(z > 0)
-        def _():
-            w_down_copy(z, c).start()
-
-        w_x_copy(0, z, c).start()
+    w_begin(1)
     c_x.wait()
 
     def x_ycopy(d):
@@ -172,35 +199,36 @@
     x_scopy(mf).start()
     v_start(0)
 
-    @pl.loop(1, n)
-    def _(d):
-        src = lax.rem(me + d, n)
-        id_copy(src, src).wait_recv()
-
-    c_ids = pltpu.make_async_copy(inbox, ids_sm, i_loc.at[0])
-    c_ids.start()
-    c_kv.wait()
-    c_ids.wait()
-
     def head_slice(h):
         return slice(h * HD, (h + 1) * HD)
 
-    @pl.loop(1, n)
-    def _(d):
-        peer = lax.rem(me + d, n)
-        want = jnp.int32(0)
+    def fill():
+        @pl.loop(1, n)
+        def _(d):
+            src = lax.rem(me + d, n)
+            id_copy(src, src).wait_recv()
+
+        c_ids = pltpu.make_async_copy(inbox, ids_sm, i_loc.at[0])
+        c_ids.start()
+        c_kv.wait()
+        c_ids.wait()
+
+        @pl.loop(1, n)
+        def _(d):
+            peer = lax.rem(me + d, n)
+            want = jnp.int32(0)
+            for j in range(tiles * topk):
+                one = ids_sm[peer, j // topk, j % topk]
+                want = jnp.where(one // mb_dev == me, lax.rem(one, mb_dev), want)
+            for h in range(heads):
+                outbox[peer, h] = kv[want, :, :, head_slice(h)]
+
+        mine = jnp.int32(0)
         for j in range(tiles * topk):
-            one = ids_sm[peer, j // topk, j % topk]
-            want = jnp.where(one // mb_dev == me, lax.rem(one, mb_dev), want)
+            one = ids_s[j // topk, j % topk]
+            mine = jnp.where(one // mb_dev == me, lax.rem(one, mb_dev), mine)
         for h in range(heads):
-            outbox[peer, h] = kv[want, :, :, head_slice(h)]
-
-    mine = jnp.int32(0)
-    for j in range(tiles * topk):
-        one = ids_s[j // topk, j % topk]
-        mine = jnp.where(one // mb_dev == me, lax.rem(one, mb_dev), mine)
-    for h in range(heads):
-        ids_in[me, h] = kv[mine, :, :, head_slice(h)]
+            ids_in[me, h] = kv[mine, :, :, head_slice(h)]
 
     def block_copy(peer, slot, h):
         return remote(
@@ -234,9 +262,10 @@
                 def _():
                     w_up_copy(z - k, c).start()
 
-                w_x_copy(0, z - k, c).start()
                 if c:
-                    v_start(nz - k)
+                    v_start(nz - k + (2 * k - nz) * ((z + 1) // nz))
+                if c == 0 or k < 2:
+                    w_x_copy(0, z - k, c).start()
 
             @pl.when(z + k < nz)
             def _():
@@ -246,10 +275,13 @@
                 def _():
                     w_down_copy(z + k, c).start()
 
-                w_x_copy(0, z + k, c).start()
                 if c:
                     v_start(k)
-
+                if c == 0 or k < 2:
+                    w_x_copy(0, z + k, c).start()
+
+        if k == 1:
+            fill()
         if k == min(2, nz - 1):
             send_blocks(range(heads), lambda pz, px: (px == xx) & inner(pz))
             for d in range(1, ny):
@@ -263,42 +295,52 @@
 
     q32[...] = jnp.zeros_like(q32)
 
-    def project(slot):
-        q32[...] += dot_nn(xf[:, pl.ds(pl.multiple_of(slot * dk, dk), dk)], wf[slot])
-
-    def send_outer():
-        send_blocks(range(heads), lambda pz, px: (px == xx) & jnp.logical_not(inner(pz)))
-
-    def by_distance(body, after=None):
-        body(z)
-        for k in range(1, nz):
-            for zz in (z - k, z + k):
-                @pl.when((zz >= 0) & (zz < nz))
-                def _():
-                    body(zz)
-            if after and k == 1:
-                after()
-
-    @pl.loop(0, nz)
-    def _(zz):
-        project(zz * nx + xx)
-
+    def project(slot, c):
+        q32[:, halves[c]] += dot_nn(
+            xf[:, pl.ds(pl.multiple_of(slot * dk, dk), dk)], wf[slot, :, halves[c]]
+        )
+
+    def at_distance(k, body):
+        for zz in (z - k, z + k) if k else (z,):
+            @pl.when((zz >= 0) & (zz < nz))
+            def _():
+                body(zz)
+
+    def arrived(r, c):
+        def body(zz):
+            w_x_arrival(r, zz, c).wait_recv()
+            if r + 1 < nx - 1:
+                w_x_copy(r + 1, zz, c).start()
+            project(zz * nx + lax.rem(xx - 1 - r + 2 * nx, nx), c)
+
+        return body
+
+    def own_column(c):
+        @pl.loop(0, nz)
+        def _(zz):
+            project(zz * nx + xx, c)
+
+    def send_outer(hs):
+        send_blocks(hs, lambda pz, px: (px == xx) & jnp.logical_not(inner(pz)))
+
+    own_column(0)
     for r in range(nx - 1):
-        def arrived(zz):
-            for c in range(2):
-                w_x_arrival(r, zz, c).wait_recv()
-                if r + 1 < nx - 1:
-                    w_x_copy(r + 1, zz, c).start()
-            project(zz * nx + lax.rem(xx - 1 - r + 2 * nx, nx))
-
-        by_distance(arrived, send_outer if r == nx - 2 else None)
-    if nx == 1:
-        send_outer()
+        for k in range(nz):
+            at_distance(k, arrived(r, 0))
+            if r == nx - 2 and k == 1:
+                send_outer(range(early))
+    for h in range(early):
+        send_crossing(h)
+    for k in range(2, nz):
+        at_distance(k, lambda zz: w_x_copy(0, zz, 1).start())
+    send_outer(range(early, heads))
+    qb[:, halves[0]] = q32[:, halves[0]].astype(jnp.bfloat16)
+
+    own_column(1)
+    for k in range(min(2, nz)):
+        at_distance(k, arrived(0, 1))
     for p in range(nz, swap):
         v_start(p)
-    send_crossing(0)
-    send_crossing(1)
-    qb[...] = q32[...].astype(jnp.bfloat16)
     c_lkv.wait()
     c_go.wait()
 
@@ -308,7 +350,7 @@
         lax.broadcasted_iota(jnp.int32, (BLK, BLK), 1)
     )
 
-    def attend(h):
+    def attend(h, then=None):
         cols = pl.ds(pl.multiple_of(h * HD, HD), HD)
 
         @pl.loop(1, n)
@@ -316,10 +358,8 @@
             src = lax.rem(me + d, n)
             block_copy(src, src, h).wait_recv()
 
-        @pl.when(h + 2 < heads)
-        def _():
-            send_crossing(h + 2)
-
+        if then:
+            then(h)
         stage[...] = ids_in[:, h]
         for t in range(tiles):
             rows = slice(t * BLK, (t + 1) * BLK)
@@ -399,46 +439,57 @@
             total = total + y_recv[d, p].astype(jnp.float32)
         return total
 
-    def g_copy(f, src, c):
-        return remote(
-            gq.at[rows_of(f), halves[c]], gq_in.at[src, :, halves[c]],
-            g_send.at[f, c], g_recv.at[src, c], me, f,
-        )
-
-    def g_start(c):
-        for d in range(1, nf):
-            g_copy(lax.rem(mf + d, nf), mf, c).start()
+    def g_copy(f, src):
+        return remote(
+            gq.at[rows_of(f), late_cols], gq_in.at[src], g_send.at[f], g_recv.at[src], me, f
+        )
+
+    def resume(h):
+        @pl.when(h == early - 1)
+        def _():
+            for late_head in range(early, heads):
+                send_crossing(late_head)
 
     @pl.loop(0, early)
     def _(h):
-        attend(h)
-
-    shares(full // per, swap // per, halves[0])
-    g_start(0)
-
-    for p in range(swap):
-        for c in v_halves(p):
-            for d in range(1, ny):
-                f = lax.rem(mf + 2 * d, nf)
-                v_fwd(f, p, c).wait_recv()
-                v_fwd(f, p, c).start()
+        attend(h, resume)
+
+    shares(0, swap // per, halves[0])
+
+    for k in range(2, nz):
+        at_distance(k, arrived(0, 1))
+    for r in range(1, nx - 1):
+        for k in range(nz):
+            at_distance(k, arrived(r, 1))
+    qb[:, late_cols] = q32[:, late_cols].astype(jnp.bfloat16)
+
+    for d in range(1, ny):
+        f = lax.rem(mf + 2 * d, nf)
+
+        @pl.loop(0, swap)
+        def _(p):
+            v_fwd(f, p).wait_recv()
+            v_fwd(f, p).start()
 
     @pl.loop(early, heads)
     def _(h):
         attend(h)
 
-    g_start(1)
+    for d in range(1, nf):
+        g_copy(lax.rem(mf + d, nf), mf).start()
+
     shares(swap // per, groups, slice(0, width))
 
-    for p in range(swap):
-        for c in v_halves(p):
-            for d in range(ny):
-                v_fwd(lax.rem(sib + 2 * d, nf), p, c).wait_recv()
+    for d in range(ny):
+        f = lax.rem(sib + 2 * d, nf)
+
+        @pl.loop(0, swap)
+        def _(p):
+            v_fwd(f, p).wait_recv()
 
     for d in range(1, nf):
         f = lax.rem(mf + d, nf)
-        for c in range(2):
-            g_copy(f, f, c).wait_recv()
+        g_copy(f, f).wait_recv()
 
     def finish(g):
         rs_s(0, g).wait_recv()
@@ -448,23 +499,19 @@
     def out_cols(p):
         return pl.ds(pl.multiple_of(slot_of(p) * dk, dk), dk)
 
-    def gathered(p, cols):
-        total = dot_nt(gq[rows_of(mf), cols], wf[slot_of(p), :, cols])
+    def gathered(p):
+        total = dot_nt(gq[rows_of(mf), late_cols], wf[slot_of(p), :, late_cols])
         for d in range(1, nf):
             f = lax.rem(mf + d, nf)
-            total = total + dot_nt(gq_in[f, :, cols], wy[f, p, :, cols])
+            total = total + dot_nt(gq_in[f], wy[f, p])
         return total
 
-    @pl.loop(0, full)
-    def _(p):
-        gin_ref[:, out_cols(p)] = gathered(p, slice(0, width)).astype(jnp.bfloat16)
-
-    @pl.loop(full // per, swap // per)
+    @pl.loop(0, swap // per)
     def _(g):
         finish(g)
         for i in range(per):
             p = g * per + i
-            gin_ref[:, out_cols(p)] = (settled(p) + gathered(p, late_cols)).astype(jnp.bfloat16)
+            gin_ref[:, out_cols(p)] = (settled(p) + gathered(p)).astype(jnp.bfloat16)
 
     @pl.loop(swap // per, groups)
     def _(g):
@@ -499,21 +546,21 @@
             x_ycopy(d).wait_send()
         x_scopy(lax.rem(mf + 2 * d, nf)).wait_send()
 
-        @pl.loop(full // per, groups)
+        @pl.loop(0, groups)
         def _(g):
             rs_s(d, g).wait_send()
             if d:
                 rs_y(d, g).wait_send()
 
-    for p in range(swap):
-        for c in v_halves(p):
-            for d in range(1, ny):
-                v_ycopy(d, p, c).wait_send()
-                v_fwd(lax.rem(mf + 2 * d, nf), p, c).wait_send()
-            v_own(p, c).wait_send()
+    @pl.loop(0, swap)
+    def _(p):
+        for d in range(1, ny):
+            v_ycopy(d, p).wait_send()
+            v_fwd(lax.rem(mf + 2 * d, nf), p).wait_send()
+        v_own(p).wait_send()
+
     for d in range(1, nf):
-        for c in range(2):
-            g_copy(lax.rem(mf + d, nf), mf, c).wait_send()
+        g_copy(lax.rem(mf + d, nf), mf).wait_send()
 
 
 def emit(a_ref, b_ref, c_ref, d_ref):
@@ -537,8 +584,8 @@
     early = heads // 2
     per = max(1, nz // 4)
     groups = n // per
-    full = nz // 2
-    swap = min(nz + per, n)
+    lw = width - early * HD
+    swap = min(nz + 2, n)
     blocks = pltpu.VMEM((n, heads, 2, BLK, HD), bf)
     piece = pltpu.VMEM((ny, n, rows_dev, dk), bf)
     outs = (
@@ -546,7 +593,7 @@
         jax.ShapeDtypeStruct((rows_dev, d_model), bf),
     )
     raw = pl.pallas_call(
-        functools.partial(kernel, n, nx, nf, mb_dev, early, per, full, swap),
+        functools.partial(kernel, n, nx, nf, mb_dev, early, per, swap),
         out_shape=outs,
         in_specs=[pl.BlockSpec(memory_space=pltpu.SMEM), vmem_spec] + [any_spec] * 5,
         out_specs=(vmem_spec, vmem_spec),
@@ -565,15 +612,15 @@
             pltpu.VMEM((ctx, width), bf),
             pltpu.VMEM((ctx, width), bf),
             pltpu.VMEM((ny, n, 2 * rows_dev, dk), bf), piece, piece, piece,
-            pltpu.VMEM((nf, swap, dk, width), bf),
-            pltpu.VMEM((nf, rows_dev, width), bf),
+            pltpu.VMEM((nf, swap, dk, lw), bf),
+            pltpu.VMEM((nf, rows_dev, lw), bf),
             dma((5,)), dma((n,)), dma((n,)), dma((1,)),
             dma((nz, 2)), dma((nz, 2)), dma((max(nx - 1, 1), nz, 2)), dma((nz, 2)),
             dma((max(nx - 1, 1), nz, 2)),
             dma((ny,)), dma((nf,)), dma((nf,)), dma((n, heads)), dma((n, heads)),
             dma((ny, groups)), dma((ny, groups)), dma((ny, groups)), dma((ny, groups)),
-            dma((ny, swap, 2)), dma((nf, swap, 2)), dma((nf, swap, 2)),
-            dma((nf, 2)), dma((nf, 2)),
+            dma((ny, swap)), dma((nf, swap)), dma((nf, swap)),
+            dma((nf,)), dma((nf,)), pltpu.SemaphoreType.REGULAR((3,)),
         ],
         compiler_params=pltpu.CompilerParams(
             collective_id=0, has_side_effects=True, vmem_limit_bytes=62 * 1024 * 1024

time: 107 us -> 103 us (0.963)
  Pallas kernels: 106 us -> 102 us
    pallas_call x1, Pallas kernels: 104 us -> 99.3 us  [local(): pl.pallas_call(functools.partial(kernel, n, nx, nf, mb_dev, early, per, s...]
where the time goes in v3:
time: 103 us; the launch traced here: 102 us
  Pallas kernels  102 us (99%)
    pallas_call x1, Pallas kernels, local(): pl.pallas_call(functools.partial(kernel, n, nx, nf, mb_dev, early, per, s...  99.3 us
    pallas_call x1, Pallas kernels, local(): return pl.pallas_call(emit, out_shape=outs)(*raw)  2.57 us

profile of v3, /device:TPU:0, one launch (start us, length us, event | category | flops | bytes accessed | tf_op | source)
XLA Modules:
  0.0 102.5 jit_solution(10715208753556047188)
XLA Ops:
  0.6 99.3 %shard_map.77 = (bf16[512,512]{1,0:T(8,128)(2,1)}, bf16[128,4096]{1,0:T(8,128)(2,1)}) custom-call(s32[4,4]{1,0:T(4,128)} %ids_v.1, s32[4,4]{1,0:T(4,128)} %ids_v.1, bf16[128,4096]{1,0:T(8,128)(2,1)} %x_hbm.1, bf16[512,512]{1,0:T(8,128)(2,1)} %w_hbm.1, bf16[2,512,512]{2,1,0:T(8,128)(2,1)} %lkv_hbm.1, bf16[16,2,128,512]{3,2,1,0:T(8,128)(2,1)} %mkv_hbm.1, ...), custom_call_target="tpu_custom_call" | custom-call | tf_op jit(solution)/shard_map/pallas_call | solution.py:595
  99.9 2.6 %shard_map.78 = (bf16[512,512]{1,0:T(8,128)(2,1)}, bf16[128,4096]{1,0:T(8,128)(2,1)}) custom-call(bf16[512,512]{1,0:T(8,128)(2,1)} %get-tuple-element.4.a_ref, bf16[128,4096]{1,0:T(8,128)(2,1)} %get-tuple-element.5.b_ref), custom_call_target="tpu_custom_call" | custom-call | tf_op jit(solution)/shard_map/pallas_call | solution.py:629

commit v4 on v3

--- a/solution.py
+++ b/solution.py
@@ -11,6 +11,7 @@
 HD = 128
 BLK = 128
 NEG_FILL = -1e30
+LAG = 3
 MESH = pl.DeviceIdType.MESH
 NT = (((1,), (1,)), ((), ()))
 
@@ -26,12 +27,12 @@
 def kernel(
     n, nx, nf, mb_dev, early, per, swap,
     ids_s, ids_v, x_hbm, w_hbm, lkv_hbm, mkv_hbm, go_hbm,
-    att_ref, gin_ref,
+    att_hbm, gin_hbm,
     wf, xf, kv, lkv, go, outbox, inbox, stage, ids_in, ids_sm, q32, qb, gq,
     part, s_recv, y_send, y_recv, wy, gq_in,
     l_sem, i_send, i_recv, i_loc, w_up, w_down, w_x, w_recv, wx_recv,
     x_ysend, x_ssend, x_recv, m_send, m_recv, r_ssend, r_srecv, r_ysend, r_yrecv,
-    v_ysend, v_ssend, v_recv, g_send, g_recv, seen,
+    v_ysend, v_ssend, v_recv, g_send, g_recv, seen, att_ref, gin_ref, o_sem,
 ):
     me = lax.axis_index("mem")
     mf = lax.axis_index("fsdp")
@@ -408,30 +409,41 @@
         )
 
     def shares(first, last, cols):
-        for d in list(range(1, ny)) + [0]:
+        def partial(d, g):
             chip = lax.rem(yy + d, ny)
             rows = pl.ds(pl.multiple_of(chip * 2 * rows_dev, 2 * rows_dev), 2 * rows_dev)
-
-            @pl.loop(first, last)
+            for i in range(per):
+                p = g * per + i
+                part[d, p] = dot_nt(gq[rows, cols], wf[slot_of(p), :, cols]).astype(
+                    jnp.bfloat16
+                )
+            rs_s(d, g).start()
+
+        def pass_on(d, g):
+            rs_s(d, g).wait_recv()
+            for i in range(per):
+                p = g * per + i
+                y_send[d, p] = (
+                    part[d, p, own_half, :].astype(jnp.float32)
+                    + s_recv[d, p].astype(jnp.float32)
+                ).astype(jnp.bfloat16)
+            rs_y(d, g).start()
+
+        lag = min(LAG, last - first)
+        for d in range(1, ny):
+            @pl.loop(first, last + lag)
             def _(g):
-                for i in range(per):
-                    p = g * per + i
-                    part[d, p] = dot_nt(gq[rows, cols], wf[slot_of(p), :, cols]).astype(
-                        jnp.bfloat16
-                    )
-                rs_s(d, g).start()
-
-        for d in range(1, ny):
-            @pl.loop(first, last)
-            def _(g):
-                rs_s(d, g).wait_recv()
-                for i in range(per):
-                    p = g * per + i
-                    y_send[d, p] = (
-                        part[d, p, own_half, :].astype(jnp.float32)
-                        + s_recv[d, p].astype(jnp.float32)
-                    ).astype(jnp.bfloat16)
-                rs_y(d, g).start()
+                @pl.when(g < last)
+                def _():
+                    partial(d, g)
+
+                @pl.when(g >= first + lag)
+                def _():
+                    pass_on(d, g - lag)
+
+        @pl.loop(first, last)
+        def _(g):
+            partial(0, g)
 
     def settled(p):
         total = part[0, p, own_half, :].astype(jnp.float32) + s_recv[0, p].astype(jnp.float32)
@@ -477,6 +489,13 @@
 
     for d in range(1, nf):
         g_copy(lax.rem(mf + d, nf), mf).start()
+    c_att = pltpu.make_async_copy(att_ref, att_hbm, o_sem.at[n])
+    c_att.start()
+
+    def out_copy(p):
+        return pltpu.make_async_copy(
+            gin_ref.at[:, out_cols(p)], gin_hbm.at[:, out_cols(p)], o_sem.at[p]
+        )
 
     shares(swap // per, groups, slice(0, width))
 
@@ -512,6 +531,7 @@
         for i in range(per):
             p = g * per + i
             gin_ref[:, out_cols(p)] = (settled(p) + gathered(p)).astype(jnp.bfloat16)
+            out_copy(p).start()
 
     @pl.loop(swap // per, groups)
     def _(g):
@@ -519,6 +539,7 @@
         for i in range(per):
             p = g * per + i
             gin_ref[:, out_cols(p)] = settled(p).astype(jnp.bfloat16)
+            out_copy(p).start()
 
     @pl.loop(1, n)
     def _(d):
@@ -561,6 +582,12 @@
 
     for d in range(1, nf):
         g_copy(lax.rem(mf + d, nf), mf).wait_send()
+
+    c_att.wait()
+
+    @pl.loop(0, n)
+    def _(p):
+        out_copy(p).wait()
 
 
 def emit(a_ref, b_ref, c_ref, d_ref):
@@ -596,7 +623,7 @@
         functools.partial(kernel, n, nx, nf, mb_dev, early, per, swap),
         out_shape=outs,
         in_specs=[pl.BlockSpec(memory_space=pltpu.SMEM), vmem_spec] + [any_spec] * 5,
-        out_specs=(vmem_spec, vmem_spec),
+        out_specs=(any_spec, any_spec),
         scratch_shapes=[
             pltpu.VMEM((n, dk, width), bf),
             pltpu.VMEM((ctx, d_model), bf),
@@ -621,6 +648,7 @@
             dma((ny, groups)), dma((ny, groups)), dma((ny, groups)), dma((ny, groups)),
             dma((ny, swap)), dma((nf, swap)), dma((nf, swap)),
             dma((nf,)), dma((nf,)), pltpu.SemaphoreType.REGULAR((3,)),
+            pltpu.VMEM((ctx, width), bf), pltpu.VMEM((rows_dev, d_model), bf), dma((n + 1,)),
         ],
         compiler_params=pltpu.CompilerParams(
             collective_id=0, has_side_effects=True, vmem_limit_bytes=62 * 1024 * 1024

time: 103 us -> 102 us (level)
  no operation moved by 1% of the time
where the time goes in v4:
time: 102 us
  Pallas kernels  101 us (99%)
    pallas_call x1, Pallas kernels, local(): pl.pallas_call(functools.partial(kernel, n, nx, nf, mb_dev, early, per, s...  98.4 us
    pallas_call x1, Pallas kernels, local(): return pl.pallas_call(emit, out_shape=outs)(*raw)  2.57 us

profile of v4, /device:TPU:0, one launch (start us, length us, event | category | flops | bytes accessed | tf_op | source)
XLA Modules:
  0.0 101.6 jit_solution(140766001875502262)
XLA Ops:
  0.6 98.4 %shard_map.77 = (bf16[512,512]{1,0:T(8,128)(2,1)}, bf16[128,4096]{1,0:T(8,128)(2,1)}) custom-call(s32[4,4]{1,0:T(4,128)} %ids_v.1, s32[4,4]{1,0:T(4,128)} %ids_v.1, bf16[128,4096]{1,0:T(8,128)(2,1)} %x_hbm.1, bf16[512,512]{1,0:T(8,128)(2,1)} %w_hbm.1, bf16[2,512,512]{2,1,0:T(8,128)(2,1)} %lkv_hbm.1, bf16[16,2,128,512]{3,2,1,0:T(8,128)(2,1)} %mkv_hbm.1, ...), custom_call_target="tpu_custom_call" | custom-call | tf_op jit(solution)/shard_map/pallas_call | solution.py:622
  99.1 2.6 %shard_map.78 = (bf16[512,512]{1,0:T(8,128)(2,1)}, bf16[128,4096]{1,0:T(8,128)(2,1)}) custom-call(bf16[512,512]{1,0:T(8,128)(2,1)} %get-tuple-element.4.a_ref, bf16[128,4096]{1,0:T(8,128)(2,1)} %get-tuple-element.5.b_ref), custom_call_target="tpu_custom_call" | custom-call | tf_op jit(solution)/shard_map/pallas_call | solution.py:657

commit v5 on v4

--- a/solution.py
+++ b/solution.py
@@ -590,9 +590,19 @@
         out_copy(p).wait()
 
 
-def emit(a_ref, b_ref, c_ref, d_ref):
-    c_ref[...] = a_ref[...]
-    d_ref[...] = b_ref[...]
+def emit(a_hbm, b_hbm, c_hbm, d_hbm, a, b, sem):
+    steps = a.shape[0]
+    jobs = []
+    for i in range(steps):
+        jobs.append((a_hbm.at[i], a.at[i], c_hbm.at[i]))
+        jobs.append((b_hbm.at[i], b.at[i], d_hbm.at[i]))
+    for j, (src, held, _) in enumerate(jobs):
+        pltpu.make_async_copy(src, held, sem.at[0, j]).start()
+    for j, (src, held, dst) in enumerate(jobs):
+        pltpu.make_async_copy(src, held, sem.at[0, j]).wait()
+        pltpu.make_async_copy(held, dst, sem.at[1, j]).start()
+    for j, (_, held, dst) in enumerate(jobs):
+        pltpu.make_async_copy(held, dst, sem.at[1, j]).wait()
 
 
 def local(n, nf, layer_input, w_query, local_kv, memory_kv, memory_ids, grad_out):
@@ -654,7 +664,16 @@
             collective_id=0, has_side_effects=True, vmem_limit_bytes=62 * 1024 * 1024
         ),
     )(memory_ids, memory_ids, layer_input, w_query, local_kv, memory_kv, grad_out)
-    return pl.pallas_call(emit, out_shape=outs)(*raw)
+    steps = 4
+    cut = [o.update(shape=(steps, o.shape[0] // steps) + o.shape[1:]) for o in outs]
+    done = pl.pallas_call(
+        emit,
+        out_shape=cut,
+        in_specs=[any_spec] * 2,
+        out_specs=[any_spec] * 2,
+        scratch_shapes=[pltpu.VMEM(c.shape, bf) for c in cut] + [dma((2, 2 * steps))],
+    )(*[r.reshape(c.shape) for r, c in zip(raw, cut)])
+    return tuple(x.reshape(o.shape) for x, o in zip(done, outs))
 
 
 def solution(mesh):

time: 102 us -> 102 us (level)
  no operation moved by 1% of the time
where the time goes in v5:
time: 102 us; the launch traced here: 101 us
  Pallas kernels  101 us (99%)
    pallas_call x1, Pallas kernels, local(): pl.pallas_call(functools.partial(kernel, n, nx, nf, mb_dev, early, per, s...  98.4 us
    pallas_call x1, Pallas kernels, local(): pl.pallas_call(emit, out_shape=cut, in_specs=[any_spec] * 2, out_specs=[a...  2.26 us

profile of v5, /device:TPU:0, one launch (start us, length us, event | category | flops | bytes accessed | tf_op | source)
XLA Modules:
  0.0 101.3 jit_solution(12185561370487541998)
XLA Ops:
  0.6 98.4 %shard_map.77 = (bf16[512,512]{1,0:T(8,128)(2,1)}, bf16[128,4096]{1,0:T(8,128)(2,1)}) custom-call(s32[4,4]{1,0:T(4,128)} %ids_v.1, s32[4,4]{1,0:T(4,128)} %ids_v.1, bf16[128,4096]{1,0:T(8,128)(2,1)} %x_hbm.1, bf16[512,512]{1,0:T(8,128)(2,1)} %w_hbm.1, bf16[2,512,512]{2,1,0:T(8,128)(2,1)} %lkv_hbm.1, bf16[16,2,128,512]{3,2,1,0:T(8,128)(2,1)} %mkv_hbm.1, ...), custom_call_target="tpu_custom_call" | custom-call | tf_op jit(solution)/shard_map/pallas_call | solution.py:632
  99.1 2.3 %shard_map.78 = (bf16[4,128,512]{2,1,0:T(8,128)(2,1)}, bf16[4,32,4096]{2,1,0:T(8,128)(2,1)}) custom-call(bf16[4,128,512]{2,1,0:T(8,128)(2,1)} %bitcast.5, bf16[4,32,4096]{2,1,0:T(8,128)(2,1)} %bitcast.4), custom_call_target="tpu_custom_call" | custom-call | tf_op jit(solution)/shard_map/pallas_call | solution.py:669

commit v6 on v5

--- a/solution.py
+++ b/solution.py
@@ -11,7 +11,7 @@
 HD = 128
 BLK = 128
 NEG_FILL = -1e30
-LAG = 3
+LAG = 2
 MESH = pl.DeviceIdType.MESH
 NT = (((1,), (1,)), ((), ()))
 

time: 102 us -> 101 us (level)
  no operation moved by 1% of the time
where the time goes in v6:
time: 101 us
  Pallas kernels  101 us (100%)
    pallas_call x1, Pallas kernels, local(): pl.pallas_call(functools.partial(kernel, n, nx, nf, mb_dev, early, per, s...  98.2 us
    pallas_call x1, Pallas kernels, local(): pl.pallas_call(emit, out_shape=cut, in_specs=[any_spec] * 2, out_specs=[a...  2.26 us

profile of v6, /device:TPU:0, one launch (start us, length us, event | category | flops | bytes accessed | tf_op | source)
XLA Modules:
  0.0 101.2 jit_solution(10879842487084558424)
XLA Ops:
  0.6 98.2 %shard_map.77 = (bf16[512,512]{1,0:T(8,128)(2,1)}, bf16[128,4096]{1,0:T(8,128)(2,1)}) custom-call(s32[4,4]{1,0:T(4,128)} %ids_v.1, s32[4,4]{1,0:T(4,128)} %ids_v.1, bf16[128,4096]{1,0:T(8,128)(2,1)} %x_hbm.1, bf16[512,512]{1,0:T(8,128)(2,1)} %w_hbm.1, bf16[2,512,512]{2,1,0:T(8,128)(2,1)} %lkv_hbm.1, bf16[16,2,128,512]{3,2,1,0:T(8,128)(2,1)} %mkv_hbm.1, ...), custom_call_target="tpu_custom_call" | custom-call | tf_op jit(solution)/shard_map/pallas_call | solution.py:632
  98.9 2.3 %shard_map.78 = (bf16[4,128,512]{2,1,0:T(8,128)(2,1)}, bf16[4,32,4096]{2,1,0:T(8,128)(2,1)}) custom-call(bf16[4,128,512]{2,1,0:T(8,128)(2,1)} %bitcast.5, bf16[4,32,4096]{2,1,0:T(8,128)(2,1)} %bitcast.4), custom_call_target="tpu_custom_call" | custom-call | tf_op jit(solution)/shard_map/pallas_call | solution.py:669
